TPU v7x, 128 devices: a whole 4x4x4 slice. The times are simulated.
128 devices in a mesh: row: 8 (over x, z_lo), sim: 16 (over y, z_hi, core).
Axes of the slice: x: 4, y: 4, z: 4 (z_hi: 2, z_lo: 2; z = z_hi * 2 + z_lo), core: 2. Of those that a mesh axis runs over, the one named last changes fastest.
Arguments:
- right_side: float32 [12288, 20480], P('row', 'sim'), may hold values from -6 to 6
- lower_panels: float32 [3, 12288, 512], P(None, ('row', 'sim')), may hold values from -0.15625 to 0.15625
- inverse_blocks: float32 [3, 512, 512], replicated, may hold values from -1 to 1.5, as said below
Outputs:
- solved: float32 [1536, 20480], P('row', 'sim')
- updated: float32 [12288, 20480], P('row', 'sim')
Inputs may be any that keep to these rules, and one draw needn't show every extreme that they name: `inverse_blocks`: each block is lower triangular with a diagonal between 0.5 and 1.5.
All inputs are finite; a program needn't handle non-finite values.
Results may differ from a plain program's by a relative error of at most 0.0001.
Values sent between devices are 32-bit elements; how exact they have to be, the bound alone decides.
No kernel may reach another device: no remote copies, remote signals or barrier semaphores. Data moves between devices by JAX's collectives and lax.ppermute only.
A program may use at most 128 MiB of HBM per device.

v0:
```python
import jax
import jax.numpy as jnp
from jax import lax
from jax.sharding import PartitionSpec as P

NB = 512
PANELS = 3


def from_root(array, axis, root):
    mine = lax.axis_index(axis) == root
    return lax.psum(jnp.where(mine, array, jnp.zeros_like(array)), axis)


def solve_block(leading, inverse, panel):
    candidate = jnp.dot(
        inverse, leading, precision=lax.Precision.HIGHEST, preferred_element_type=jnp.float32
    )
    return from_root(candidate, "row", panel)


def local(right_side, lower_panels, inverse_blocks):
    row_count = lax.axis_size("row")
    row_index = lax.axis_index("row")
    local_rows = right_side.shape[0]
    row_block = jnp.arange(local_rows) // NB * row_count + row_index
    solved_list = []
    for panel in range(PANELS):
        solved_block = solve_block(right_side[:NB], inverse_blocks[panel], panel)
        solved_list.append(solved_block)
        change = jnp.dot(
            lax.all_gather(lower_panels[panel], "sim", axis=0, tiled=True),
            solved_block,
            precision=lax.Precision.HIGHEST,
            preferred_element_type=jnp.float32,
        )
        keeping = (row_block > panel).astype(jnp.float32)[:, None]
        right_side = right_side - keeping * change
    stacked = jnp.concatenate(solved_list, 0)
    share = stacked.shape[0] // row_count
    solved = lax.dynamic_slice_in_dim(stacked, row_index * share, share, 0)
    return (solved, right_side)


def solution(mesh):
    placed = (P("row", "sim"), P(None, ("row", "sim"), None), P())
    return jax.shard_map(
        local,
        mesh=mesh,
        in_specs=placed,
        out_specs=(P("row", "sim"), P("row", "sim")),
        check_vma=False,
    )
```

profile of v0, /device:TPU:13, one launch (start us, length us, event | category | flops | bytes accessed | tf_op | source)
XLA Modules:
  0.0 548.2 jit_solution(3076437522991937851)
XLA Ops:
  8.0 0.0 all-reduce.4.cloned.1.call-start
  8.1 8.1 %convolution_select_fusion.2 = f32[512,1280]{1,0:T(8,128)} fusion(f32[1536,1280]{1,0:T(8,128)} %param.3, pred[]{:T(512)S(6)} %eq.9, f32[3,512,512]{2,1,0:T(8,128)} %param.5), kind=kOutput, calls=%fused_computation.14 | convolution fusion | flops 4027187200 | bytes 6291457 | tf_op jit(solution)/shard_map/dot_general | solution.py:16
  16.1 0.0 all-reduce.4.cloned.1.call-update
  16.2 0.0 all-gather.7.cloned.1.call-start
  16.2 0.0 copy-done.4
  16.2 0.8 fusion.33
  17.0 0.0 all-gather.7.cloned.1.call-update
  17.1 0.0 all-gather.9.cloned.1.call-start
  17.1 0.5 all-gather.9.cloned.1.call-update
  17.7 0.0 all-reduce.6.cloned.1.call-start
  17.7 9.1 %copy.5 = f32[1536,1280]{0,1:T(8,128)} copy(f32[1536,1280]{1,0:T(8,128)} %param.3) | data formatting | bytes 15728640 | tf_op args[0]
  26.8 134.8 %all-reduce.4.cloned.1.call-done = f32[512,1280]{1,0:T(8,128)} async-done(((f32[512,1280]{1,0:T(8,128)}), f32[512,1280]{1,0:T(8,128)}) %all-reduce.4.cloned.1.call-update) | async-done | bytes 2621456 | tf_op jit(solution)/shard_map/psum | solution.py:12
  161.6 29.4 %fusion.1 = f32[1536,1280]{0,1:T(8,128)S(1)} fusion(f32[1536,1280]{0,1:T(8,128)} %copy.5, f32[512,1280]{1,0:T(8,128)} %all-reduce.4.cloned.1.call-done, f32[1536]{0:T(1024)S(1)} %fusion.29, f32[1,1536,512]{2,1,0:T(8,128)} %all-gather.7.cloned.1.call-done), kind=kOutput, calls=%fused_computation.4 | convolution fusion | flops 12083527680 | bytes 21501952 | tf_op jit(solution)/shard_map/dot_general | solution.py:31
  191.1 0.0 copy-start
  191.1 3.2 copy-done
  194.3 5.9 %fusion.6 = f32[512,1280]{1,0:T(8,128)} fusion(f32[1536,1280]{0,1:T(8,128)S(1)} %fusion.1, pred[]{:T(512)S(6)} %eq.10, f32[3,512,512]{2,1,0:T(8,128)S(1)} %copy-done.3), kind=kOutput, calls=%fused_computation.15 | convolution fusion | flops 4027187200 | bytes 6291457 | tf_op jit(solution)/shard_map/dot_general | solution.py:16
  200.2 0.0 all-reduce.6.cloned.1.call-update
  200.2 0.0 all-gather.11.cloned.1.call-start
  200.3 0.5 all-gather.11.cloned.1.call-update
  200.8 0.0 all-reduce.8.cloned.1.call-start
  200.9 0.0 all-gather.9.cloned.1.call-done
  200.9 134.8 %all-reduce.6.cloned.1.call-done = f32[512,1280]{1,0:T(8,128)} async-done(((f32[512,1280]{1,0:T(8,128)}), f32[512,1280]{1,0:T(8,128)}) %all-reduce.6.cloned.1.call-update) | async-done | bytes 2621456 | tf_op jit(solution)/shard_map/psum | solution.py:12
  335.7 28.9 %fusion.3 = f32[1536,1280]{0,1:T(8,128)S(1)} fusion(f32[1536,1280]{0,1:T(8,128)} %copy-done, f32[512,1280]{1,0:T(8,128)} %all-reduce.6.cloned.1.call-done, f32[1536]{0:T(1024)S(1)} %fusion.30, f32[1,1536,512]{2,1,0:T(8,128)} %all-gather.9.cloned.1.call-done), kind=kOutput, calls=%fused_computation.6 | convolution fusion | flops 12083527680 | bytes 21501952 | tf_op jit(solution)/shard_map/dot_general | solution.py:31
  364.7 0.0 copy-start.1
  364.7 3.2 copy-done.1
  367.9 5.9 %fusion.7 = f32[512,1280]{1,0:T(8,128)} fusion(f32[1536,1280]{0,1:T(8,128)S(1)} %fusion.3, pred[]{:T(512)S(6)} %eq.11, f32[3,512,512]{2,1,0:T(8,128)S(1)} %copy-done.3), kind=kOutput, calls=%fused_computation.16 | convolution fusion | flops 4027187200 | bytes 6291457 | tf_op jit(solution)/shard_map/dot_general | solution.py:16
  373.8 0.0 all-reduce.8.cloned.1.call-update
  373.8 0.0 all-gather.11.cloned.1.call-done
  373.8 125.7 %all-reduce.8.cloned.1.call-done = f32[512,1280]{1,0:T(8,128)} async-done(((f32[512,1280]{1,0:T(8,128)}), f32[512,1280]{1,0:T(8,128)}) %all-reduce.8.cloned.1.call-update) | async-done | bytes 2621456 | tf_op jit(solution)/shard_map/psum | solution.py:12
  499.6 29.4 %fusion.5 = f32[1536,1280]{0,1:T(8,128)} fusion(f32[1536,1280]{0,1:T(8,128)} %copy-done.1, f32[512,1280]{1,0:T(8,128)} %all-reduce.8.cloned.1.call-done, f32[1536]{0:T(1024)S(1)} %fusion.31, f32[1,1536,512]{2,1,0:T(8,128)} %all-gather.11.cloned.1.call-done), kind=kOutput, calls=%fused_computation.8 | convolution fusion | flops 12083527680 | bytes 21501952 | tf_op jit(solution)/shard_map/dot_general | solution.py:31
  529.0 9.2 %copy.8 = f32[1536,1280]{1,0:T(8,128)} copy(f32[1536,1280]{0,1:T(8,128)} %fusion.5) | data formatting | bytes 15728640
  538.2 2.5 fusion.21
  (9 shorter events, 0.0 us)
Async XLA Ops:
  8.0 153.6 %all-reduce.4.cloned.1.call-start = ((), (), s32[]{:S(2)}) async-start(), calls=%async_computation | async-start | bytes 5242880 | tf_op jit(solution)/shard_map/psum | solution.py:12
  8.0 8.2 %copy-start.4 = (f32[3,96,512]{2,1,0:T(8,128)S(1)}, f32[3,96,512]{2,1,0:T(8,128)}, u32[]{:S(2)}) copy-start(f32[3,96,512]{2,1,0:T(8,128)} %param.4) | copy-start | bytes 1769476
  16.2 145.5 %all-gather.7.cloned.1.call-start = ((), (), s32[]{:S(2)}) async-start(), calls=%async_computation.3 | async-start | bytes 3342336 | tf_op jit(solution)/shard_map/all_gather | solution.py:32
  17.1 183.8 %all-gather.9.cloned.1.call-start = ((), (), s32[]{:S(2)}) async-start(), calls=%async_computation.4 | async-start | bytes 3342336 | tf_op jit(solution)/shard_map/all_gather | solution.py:32
  17.7 318.1 %all-reduce.6.cloned.1.call-start = ((), (), s32[]{:S(2)}) async-start(), calls=%async_computation.1 | async-start | bytes 5242880 | tf_op jit(solution)/shard_map/psum | solution.py:12
  26.8 167.5 %copy-start.3 = (f32[3,512,512]{2,1,0:T(8,128)S(1)}, f32[3,512,512]{2,1,0:T(8,128)}, u32[]{:S(2)}) copy-start(f32[3,512,512]{2,1,0:T(8,128)} %param.5) | copy-start | bytes 9437188
  191.1 3.2 copy-start
  200.2 173.6 %all-gather.11.cloned.1.call-start = ((), (), s32[]{:S(2)}) async-start(), calls=%async_computation.5 | async-start | bytes 3342336 | tf_op jit(solution)/shard_map/all_gather | solution.py:32
  200.8 298.8 %all-reduce.8.cloned.1.call-start = ((), (), s32[]{:S(2)}) async-start(), calls=%async_computation.2 | async-start | bytes 5242880 | tf_op jit(solution)/shard_map/psum | solution.py:12
  364.7 3.2 copy-start.1
  529.0 9.2 %copy-start.2 = (f32[512,1280]{1,0:T(8,128)S(1)}, f32[512,1280]{1,0:T(8,128)}, u32[]{:S(2)}) copy-start(f32[512,1280]{1,0:T(8,128)} %all-reduce.4.cloned.1.call-done) | copy-start | bytes 7864324
Sparse Core Ops, SparseCore 0:
  16.3 145.2 all-reduce.3
  200.3 135.3 all-reduce.5
  373.9 125.6 all-reduce.7
Sparse Core Ops, SparseCore 1:
  19.0 64.9 all-gather.6
  86.3 58.5 all-gather.8
  203.7 62.8 all-gather.10
where the time goes:
time: 553 us; the launch traced here: 548 us
  waiting for transfers between devices  397 us (72%)
  matrix products  108 us (20%)
  local copies, waits for them, and re-layouts  25.5 us (5%)
  between operations  15.7 us (3%)
    psum x3, waiting for transfers between devices, from_root(): return lax.psum(jnp.where(mine, array, jnp.zeros_like(array)), axis)  395 us
    dot_general x3, matrix products, local(): jnp.dot(lax.all_gather(lower_panels[panel], 'sim', axis=0, tiled=True), s...  87.8 us
    unnamed x12, local copies, waits for them, and re-layouts  24.7 us
    dot_general x3, matrix products, solve_block(): jnp.dot(inverse, leading, precision=lax.Precision.HIGHEST, preferred_elem...  19.9 us
  transfers between devices with their start and end apart: 6, of which 3 were waited for; matrix products, arithmetic and copies ran while one was open for 15% of the time, Pallas kernels for 0%

commit v1 on v0

v1 whole, which is shorter than its diff:
```python
import jax
import jax.numpy as jnp
from jax import lax
from jax.experimental import pallas as pl
from jax.experimental.pallas import tpu as pltpu
from jax.sharding import PartitionSpec as P


NB = 512
PANELS = 3
MAIN, REST = 128, 32
PIECE = MAIN + REST
HALF = PIECE // 2
DEPTH = PANELS * NB
AXES = ("row", "sim")
NT = (((1,), (1,)), ((), ()))


def index_of(x, zl, y, zh, c):
    return (x % 4 * 2 + zl) * 16 + (y % 4 * 4 + zh * 2 + c)


def pairs_of(move):
    pairs = []
    for x in range(4):
        for zl in range(2):
            for y in range(4):
                for zh in range(2):
                    for c in range(2):
                        pairs.append((index_of(x, zl, y, zh, c), index_of(*move(x, zl, y, zh, c))))
    return pairs


X_UP = pairs_of(lambda x, zl, y, zh, c: (x + 1, zl, y, zh, c))
X_DOWN = pairs_of(lambda x, zl, y, zh, c: (x - 1, zl, y, zh, c))
Y_UP = pairs_of(lambda x, zl, y, zh, c: (x, zl, y + 1, zh, c))
Y_DOWN = pairs_of(lambda x, zl, y, zh, c: (x, zl, y - 1, zh, c))
Z_SWAP = pairs_of(lambda x, zl, y, zh, c: (x, 1 - zl, y, zh, c))
FAR_SWAP = pairs_of(lambda x, zl, y, zh, c: (x, zl, y, 1 - zh, c))
CORE_SWAP = pairs_of(lambda x, zl, y, zh, c: (x, zl, y, zh, 1 - c))


def send(array, pairs):
    return lax.ppermute(array, AXES, pairs)


def split(x):
    hi = x.astype(jnp.bfloat16)
    return hi, (x - hi.astype(jnp.float32)).astype(jnp.bfloat16)


def dot3(a, b):
    (ah, al), (bh, bl) = a, b
    dot = lambda u, v: lax.dot_general(u, v, NT, preferred_element_type=jnp.float32)
    return (dot(ah, bl) + dot(al, bh)) + dot(ah, bh)


def spread_rows(lower_panels):
    zeros = jnp.zeros((32, NB), jnp.float32)
    row = lax.axis_index("row")
    held = None
    for k in range(3):
        pairs = [(r * 16 + s, r * 16 + 3 * s + k) for r in (1, 2) for s in range(6) if 3 * s + k < 16]
        got = send(lower_panels[:2, 32 * k : 32 * k + 32], pairs)
        held = got if held is None else held + got
    first = jnp.where(row == 1, held[0], 0.0)
    others = jnp.where(row == 2, held, 0.0)
    rows = jnp.concatenate([first, others[0], others[1]], 0)
    beside = send(rows, [(a, b) for a, b in Z_SWAP if a // 16 in (1, 2)])
    rows = rows + beside
    total = rows
    for k in (1, 2, 3):
        pairs = [((x * 2 + z) * 16 + s, ((x + k) % 4 * 2 + z) * 16 + s) for x in (0, 1) for z in (0, 1) for s in range(16)]
        total = total + send(rows, pairs)
    return total


def over_sim(own):
    far = send(own, FAR_SWAP)
    up, down = send(own, Y_UP), send(own, Y_DOWN)
    g1 = jnp.stack([own, up, down])
    far_up, far_down = send(far, Y_UP), send(far, Y_DOWN)
    g2 = jnp.stack([far, far_up, far_down])
    g3 = jnp.stack([send(up, Y_UP), send(far_down, Y_DOWN)])
    return [g for group in (g1, g2, g3) for g in (group, send(group, CORE_SWAP))]


GROUPS = (
    (((0, 0), (3, 0), (1, 0)), 0), (((0, 0), (3, 0), (1, 0)), 1),
    (((0, 1), (3, 1), (1, 1)), 0), (((0, 1), (3, 1), (1, 1)), 1),
    (((2, 0), (2, 1)), 0), (((2, 0), (2, 1)), 1),
)
SMEM = pl.BlockSpec(memory_space=pltpu.SMEM)
VMEM = pl.BlockSpec(memory_space=pltpu.VMEM)


def members(where_ref, refs):
    y, zh, core = where_ref[2], where_ref[3], where_ref[4]
    for (steps, other), ref in zip(GROUPS, refs):
        c = 1 - core if other else core
        for i, (step, flip) in enumerate(steps):
            z = 1 - zh if flip else zh
            yield ref.at[i], lax.rem(y + step, 4) * 4 + z * 2 + c


def turn_kernel(b_ref, o_ref):
    for d in range(8):
        o_ref[d, :MAIN] = b_ref[:, MAIN * d : MAIN * d + MAIN].T
    rest = b_ref[:, 8 * MAIN :].T
    for d in range(8):
        o_ref[d, MAIN:] = rest[REST * d : REST * d + REST]


def turn(right_side):
    return pl.pallas_call(
        turn_kernel,
        grid=(1,),
        out_shape=jax.ShapeDtypeStruct((8, PIECE, NB), jnp.float32),
        in_specs=[pl.BlockSpec((NB, 1280), lambda i: (0, 0))],
        out_specs=pl.BlockSpec((8, PIECE, NB), lambda i: (0, 0, 0)),
        compiler_params=pltpu.CompilerParams(vmem_limit_bytes=20 << 20),
        cost_estimate=pl.CostEstimate(flops=0, bytes_accessed=5 << 20, transcendentals=0),
        name="turn",
    )(right_side)


def solve_kernel(where_ref, pieces_ref, *refs):
    groups, (inverse_ref, y_ref, wh, wl) = refs[:6], refs[6:]
    for ref, s in members(where_ref, groups):
        rows = pl.ds(pl.multiple_of(s * 32, 32), 32)
        for k in range(3):
            hi, lo = split(ref[32 * k : 32 * k + 32])
            wh[k, rows, :] = hi
            wl[k, rows, :] = lo
    window = lambda k: (wh[k], wl[k])
    y0 = dot3(split(pieces_ref[0]), split(inverse_ref[0]))
    y_ref[:, :NB] = y0
    y0 = split(y0)
    y1 = dot3(split(pieces_ref[1] - dot3(y0, window(0))), split(inverse_ref[1]))
    y_ref[:, NB : 2 * NB] = y1
    y1 = split(y1)
    rest = pieces_ref[2] - dot3(y0, window(1)) - dot3(y1, window(2))
    y_ref[:, 2 * NB :] = dot3(split(rest), split(inverse_ref[2]))


def solve(where, pieces, groups, inverse_blocks):
    whole = lambda p: pl.BlockSpec(p.shape, lambda i: (0,) * len(p.shape))
    return pl.pallas_call(
        solve_kernel,
        grid=(1,),
        out_shape=jax.ShapeDtypeStruct((PIECE, DEPTH), jnp.float32),
        in_specs=[SMEM, pl.BlockSpec((3, PIECE, NB), lambda i: (0, 0, 0))] + [whole(p) for p in (*groups, inverse_blocks)],
        out_specs=pl.BlockSpec((PIECE, DEPTH), lambda i: (0, 0)),
        scratch_shapes=[pltpu.VMEM((3, NB, NB), jnp.bfloat16)] * 2,
        compiler_params=pltpu.CompilerParams(vmem_limit_bytes=30 << 20),
        cost_estimate=pl.CostEstimate(flops=36 * PIECE * NB * NB, bytes_accessed=9 << 20, transcendentals=0),
        name="solve",
    )(where, pieces, *groups, inverse_blocks)


def factor_kernel(where_ref, *refs):
    groups, (h_ref, l_ref) = refs[:6], refs[6:]
    row = where_ref[0]
    for ref, s in members(where_ref, groups):
        first = pl.multiple_of(s * 96, 32)
        rows = pl.ds(first, 96)
        index = first + lax.broadcasted_iota(jnp.int32, (96, NB), 0)
        for k in range(PANELS):
            keep = jnp.logical_or(index >= NB, row > k)
            hi, lo = split(jnp.where(keep, ref[k], 0.0))
            h_ref[rows, k * NB : k * NB + NB] = hi
            l_ref[rows, k * NB : k * NB + NB] = lo


def prepare_factor(where, groups):
    shape = jax.ShapeDtypeStruct((DEPTH, DEPTH), jnp.bfloat16)
    return pl.pallas_call(
        factor_kernel,
        out_shape=(shape, shape),
        in_specs=[SMEM] + [VMEM] * 6,
        out_specs=(VMEM, VMEM),
        compiler_params=pltpu.CompilerParams(vmem_limit_bytes=30 << 20),
        cost_estimate=pl.CostEstimate(flops=4 * DEPTH * DEPTH, bytes_accessed=8 * DEPTH * DEPTH, transcendentals=0),
        name="factor",
    )(where, *groups)


TILE = 512


def put(raw, block, first, ref, rows):
    raw[block, pl.ds(pl.multiple_of(first, 16), rows.stop - rows.start), :] = ref[rows, :]


def update_kernel(fill, where_ref, *refs):
    pieces, (fh, fl, b_ref, _, _, o_ref, s_ref, raw, yh, yl) = refs[:-10], refs[-10:]
    tile, block = pl.program_id(0), pl.program_id(1)

    @pl.when(jnp.logical_and(tile == 0, block == 0))
    def _():
        fill(where_ref, pieces, raw)

    @pl.when(tile == 0)
    def _():
        hi, lo = split(raw[block])
        yh[block] = hi
        yl[block] = lo
        x, z = where_ref[5], where_ref[1]
        start = pl.multiple_of(x * 384 + z * 128, 128)
        turned = raw[block, :, pl.ds(start, 256)].T
        s_ref[...] = jnp.where(z == 0, turned[:192], turned[64:])

    o_ref[...] = b_ref[...] - dot3((fh[...], fl[...]), (yh[block], yl[block]))


def update(blocks, fill, place, where, pieces, factor, right_side, targets):
    whole = lambda p: pl.BlockSpec(p.shape, lambda i, j, w: (0,) * len(p.shape), pipeline_mode=pl.Buffered(1))
    column = pl.BlockSpec((TILE, 256), lambda i, j, w: (i, place(j, w)))
    once = pl.BlockSpec((192, 256), lambda i, j, w: (0, place(jnp.where(i == 0, j, blocks - 1), w)))
    tall = pl.BlockSpec((TILE, DEPTH), lambda i, j, w: (i, 0))
    body = lambda *refs: update_kernel(fill, *refs)
    operands = [where, *pieces, *factor, right_side]
    specs = [whole(p) for p in pieces] + [tall, tall, column]
    aliases = {}
    if targets is None:
        targets = (jnp.zeros((8, 128), jnp.float32),) * 2
    else:
        aliases = {len(operands): 0, len(operands) + 1: 1}
    operands += targets
    specs += [pl.BlockSpec(memory_space=pl.ANY)] * 2
    return pl.pallas_call(
        body,
        out_shape=(jax.ShapeDtypeStruct((1536, 1280), jnp.float32), jax.ShapeDtypeStruct((192, 1280), jnp.float32)),
        grid_spec=pltpu.PrefetchScalarGridSpec(
            num_scalar_prefetch=1,
            grid=(1536 // TILE, blocks),
            in_specs=specs,
            out_specs=(column, once),
            scratch_shapes=[pltpu.VMEM((blocks, 256, DEPTH), d) for d in (jnp.float32, jnp.bfloat16, jnp.bfloat16)],
        ),
        input_output_aliases=aliases,
        compiler_params=pltpu.CompilerParams(vmem_limit_bytes=44 << 20),
        cost_estimate=pl.CostEstimate(
            flops=6 * DEPTH * DEPTH * 256 * blocks,
            bytes_accessed=4 * DEPTH * DEPTH + 3072 * 1024 * blocks, transcendentals=0,
        ),
        name="update",
    )(*operands)


A, B = slice(0, HALF), slice(HALF, PIECE)


def fill_near(where, pieces, raw):
    z = where[1]
    mine, beside = pieces
    put(raw, 0, z * MAIN, mine, slice(0, MAIN))
    put(raw, 0, (1 - z) * MAIN, beside, slice(0, MAIN))


def fill_sides(where, pieces, raw):
    z = where[1]
    left, right, crossed, up, down = pieces
    put(raw, 0, z * MAIN, left, slice(0, MAIN))
    put(raw, 1, z * MAIN, right, slice(0, MAIN))
    other = (1 - z) * MAIN
    put(raw, 0, other, crossed, slice(0, HALF))
    put(raw, 0, other + HALF, up, slice(HALF, MAIN))
    put(raw, 1, other, down, slice(HALF, PIECE))
    put(raw, 1, other + HALF, crossed, slice(HALF, MAIN))


def fill_last(where, pieces, raw):
    x, z = where[5], where[1]
    mine, beside, left, right, crossed, up, down, far_a, far_b = pieces
    put(raw, 0, z * MAIN, up, slice(0, HALF))
    put(raw, 0, z * MAIN + HALF, down, slice(0, MAIN - HALF))
    other = (1 - z) * MAIN
    put(raw, 0, other, far_a, slice(0, HALF))
    put(raw, 0, other + HALF, far_b, slice(0, MAIN - HALF))
    tails = (
        (0, 0, mine, MAIN), (0, 1, beside, MAIN), (3, 0, left, MAIN), (1, 0, right, MAIN),
        (3, 1, up, MAIN), (1, 1, crossed, MAIN), (2, 0, down, MAIN - HALF), (2, 1, far_b, MAIN - HALF),
    )
    for dx, dz, ref, first in tails:
        owner = lax.rem(x + dx, 4) * 2 + (z if dz == 0 else 1 - z)
        put(raw, 1, owner * REST, ref, slice(first, first + REST))


def work(right_side, lower_panels, inverse_blocks):
    row, sim = lax.axis_index("row"), lax.axis_index("sim")
    where = jnp.stack([row, row % 2, sim // 4, sim // 2 % 2, sim % 2, row // 2]).astype(jnp.int32)

    rows = spread_rows(lower_panels)
    window = over_sim(rows)
    factor = prepare_factor(where, over_sim(lower_panels))

    payload = turn(right_side)
    pieces = lax.all_to_all(payload, "row", 0, 0)
    mine = solve(where, pieces, window, inverse_blocks)

    left, right, beside = send(mine, X_UP), send(mine, X_DOWN), send(mine, Z_SWAP)
    crossed = send(jnp.concatenate([left[A], right[B]], 0), Z_SWAP)
    up = send(jnp.concatenate([left[A], beside[B]], 0), X_UP)
    down = send(jnp.concatenate([right[B], beside[A]], 0), X_DOWN)
    far_a, far_b = send(crossed[A], X_UP), send(crossed[B], X_DOWN)

    done = update(1, fill_near, lambda j, w: w[5], where, (mine, beside), factor, right_side, None)
    done = update(
        2, fill_sides, lambda j, w: lax.rem(w[5] + 3 + 2 * j, 4), where, (left, right, crossed, up, down),
        factor, right_side, done,
    )
    done = update(
        2, fill_last, lambda j, w: jnp.where(j == 0, lax.rem(w[5] + 2, 4), 4), where,
        (mine, beside, left, right, crossed, up, down, far_a, far_b), factor, right_side, done,
    )
    return done[1], done[0]


def solution(mesh):
    placed = (P("row", "sim"), P(None, ("row", "sim"), None), P())
    return jax.shard_map(
        work, mesh=mesh, in_specs=placed, out_specs=(P("row", "sim"), P("row", "sim")), check_vma=False
    )
```

time: 553 us -> 209 us (0.38)
  the two profiles are of different devices: /device:TPU:13 before, /device:TPU:32 now
where the time goes in v1:
time: 209 us; the launch traced here: 208 us
  waiting for transfers between devices  92.6 us (44%)
  starting transfers between devices  50.8 us (24%)
  Pallas kernels  47 us (22%)
  local copies, waits for them, and re-layouts  10.5 us (5%)
  other arithmetic  6.6 us (3%)
    ppermute x35, waiting for transfers between devices, send(): return lax.ppermute(array, AXES, pairs)  92.6 us
    ppermute x35, starting transfers between devices, send(): return lax.ppermute(array, AXES, pairs)  47 us
    pallas_call x3, Pallas kernels, update(): pl.pallas_call(body, out_shape=(jax.ShapeDtypeStruct((1536, 1280), jnp.fl...  36.4 us
    unnamed x12, local copies, waits for them, and re-layouts  9.17 us
    pallas_call x1, Pallas kernels, solve(): pl.pallas_call(solve_kernel, grid=(1,), out_shape=jax.ShapeDtypeStruct((P...  5.33 us
  transfers between devices with their start and end apart: 36, of which 14 were waited for; matrix products, arithmetic and copies ran while one was open for 3% of the time, Pallas kernels for 16%

profile of v1, /device:TPU:32, one launch (start us, length us, event | category | flops | bytes accessed | tf_op | source)
XLA Modules:
  0.0 208.4 jit_solution(12969924823098691752)
XLA Ops:
  3.5 6.1 %collective-permute-start.2 = (f32[2,32,512]{2,1,0:T(8,128)S(1)}, f32[2,32,512]{2,1,0:T(8,128)S(1)}, u32[]{:S(2)}, u32[]{:S(2)}) collective-permute-start(f32[2,32,512]{2,1,0:T(8,128)S(1)} %get-tuple-element.25), channel_id=1, source_target_pairs={{16,18},{17,21},{18,24},{19,27},{20,30},{32,34},{33,37},{34,40},{3... | collective-permute-start | bytes 393224 | tf_op jit(solution)/shard_map/ppermute | solution.py:44
  10.2 3.2 %copy-done = f32[1536,1280]{1,0:T(8,128)S(1)} copy-done((f32[1536,1280]{1,0:T(8,128)S(1)}, f32[1536,1280]{1,0:T(8,128)}, u32[]{:S(2)}) %copy-start) | copy-done | bytes 7864344
  13.4 2.2 %turn.1 = f32[8,160,512]{2,1,0:T(8,128)} custom-call(f32[1536,1280]{1,0:T(8,128)S(1)} %copy-done), custom_call_target="tpu_custom_call" | custom-call | bytes 5242880 | tf_op jit(solution)/shard_map/turn/pallas_call | solution.py:115
  15.7 3.8 %all-to-all-start = ((f32[8,160,512]{2,1,0:T(8,128)}), f32[8,160,512]{2,1,0:T(8,128)S(1)}, u32[]{:S(2)}, u32[]{:S(2)}) async-start(f32[8,160,512]{2,1,0:T(8,128)} %turn.1), calls=%async_computation | async-start | bytes 5242880 | tf_op jit(solution)/shard_map/all_to_all | solution.py:299
  19.6 1.9 collective-permute-start.3
  21.5 29.8 %collective-permute-done.3 = f32[96,512]{1,0:T(8,128)S(1)} collective-permute-done((f32[96,512]{1,0:T(8,128)S(1)}, f32[96,512]{1,0:T(8,128)S(1)}, u32[]{:S(2)}, u32[]{:S(2)}) %collective-permute-start.3) | collective-permute-done | bytes 196640 | tf_op jit(solution)/shard_map/ppermute | solution.py:44
  51.4 1.9 collective-permute-start.6
  54.6 4.8 %collective-permute-start.4 = (f32[96,512]{1,0:T(8,128)S(1)}, f32[96,512]{1,0:T(8,128)S(1)}, u32[]{:S(2)}, u32[]{:S(2)}) collective-permute-start(f32[96,512]{1,0:T(8,128)S(1)} %fusion.1), channel_id=1, source_target_pairs={{0,32},{1,33},{2,34},{3,35},{4,36},{5,37},{6,38},{7,39},{8,40},{9,... | collective-permute-start | bytes 589832 | tf_op jit(solution)/shard_map/ppermute | solution.py:44
  59.4 2.5 %collective-permute-done.6 = f32[96,512]{1,0:T(8,128)S(1)} collective-permute-done((f32[96,512]{1,0:T(8,128)S(1)}, f32[96,512]{1,0:T(8,128)S(1)}, u32[]{:S(2)}, u32[]{:S(2)}) %collective-permute-start.6) | collective-permute-done | bytes 196640 | tf_op jit(solution)/shard_map/ppermute | solution.py:44
  61.9 2.5 %collective-permute-done.4 = f32[96,512]{1,0:T(8,128)S(1)} collective-permute-done((f32[96,512]{1,0:T(8,128)S(1)}, f32[96,512]{1,0:T(8,128)S(1)}, u32[]{:S(2)}, u32[]{:S(2)}) %collective-permute-start.4) | collective-permute-done | bytes 196640 | tf_op jit(solution)/shard_map/ppermute | solution.py:44
  64.4 2.0 collective-permute-start.10
  66.5 2.0 collective-permute-start.7
  70.1 2.9 %collective-permute-done.10 = f32[96,512]{1,0:T(8,128)S(1)} collective-permute-done((f32[96,512]{1,0:T(8,128)S(1)}, f32[96,512]{1,0:T(8,128)S(1)}, u32[]{:S(2)}, u32[]{:S(2)}) %collective-permute-start.10) | collective-permute-done | bytes 196640 | tf_op jit(solution)/shard_map/ppermute | solution.py:44
  73.0 2.0 collective-permute-start.11
  75.1 3.5 %collective-permute-done.12 = f32[96,512]{1,0:T(8,128)S(1)} collective-permute-done((f32[96,512]{1,0:T(8,128)S(1)}, f32[96,512]{1,0:T(8,128)S(1)}, u32[]{:S(2)}, u32[]{:S(2)}) %collective-permute-start.12) | collective-permute-done | bytes 196640 | tf_op jit(solution)/shard_map/ppermute | solution.py:44
  78.6 3.3 %collective-permute-done.11 = f32[96,512]{1,0:T(8,128)S(1)} collective-permute-done((f32[96,512]{1,0:T(8,128)S(1)}, f32[96,512]{1,0:T(8,128)S(1)}, u32[]{:S(2)}, u32[]{:S(2)}) %collective-permute-start.11) | collective-permute-done | bytes 196640 | tf_op jit(solution)/shard_map/ppermute | solution.py:44
  82.8 13.6 %collective-permute-done.14 = f32[96,512]{1,0:T(8,128)S(1)} collective-permute-done((f32[96,512]{1,0:T(8,128)S(1)}, f32[96,512]{1,0:T(8,128)S(1)}, u32[]{:S(2)}, u32[]{:S(2)}) %collective-permute-start.14) | collective-permute-done | bytes 196640 | tf_op jit(solution)/shard_map/ppermute | solution.py:44
  100.8 2.0 collective-permute-start.29
  105.7 5.3 %solve.1.refs_1_ = f32[160,1536]{1,0:T(8,128)S(1)} custom-call(s32[6]{0:T(128)S(1)} %stack.93.where_ref.refs_0_, f32[8,160,512]{2,1,0:T(8,128)S(1)} %all-to-all-done.pieces_ref, f32[3,96,512]{2,1,0:T(8,128)S(1)} %pad_maximum_fusion.6.refs_0_, f32[3,96,512]{2,1,0:T(8,128)S(1)} %copy-done.5, f32[3,96,512]{2,1,0:T(8,128)} %pad_maximum_fusion.7.refs_2_, ...), custom_call_target="tpu_custom_call" | custom-call | flops 1509949440 | bytes 9437184 | tf_op jit(solution)/shard_map/solve/pallas_call | solution.py:148
  111.0 3.2 %collective-permute-start.17 = (f32[160,1536]{1,0:T(8,128)S(1)}, f32[160,1536]{1,0:T(8,128)S(1)}, u32[]{:S(2)}, u32[]{:S(2)}) collective-permute-start(f32[160,1536]{1,0:T(8,128)S(1)} %solve.1.refs_1_), channel_id=1, source_target_pairs={{0,16},{1,17},{2,18},{3,19},{4,20},{5,21},{6,22},{7,23},{8,24},{9,... | collective-permute-start | bytes 2949128 | tf_op jit(solution)/shard_map/ppermute | solution.py:44
  115.5 11.4 %collective-permute-done.26 = f32[3,96,512]{2,1,0:T(8,128)} collective-permute-done((f32[3,96,512]{2,1,0:T(8,128)}, f32[3,96,512]{2,1,0:T(8,128)}, u32[]{:S(2)}, u32[]{:S(2)}) %collective-permute-start.26) | collective-permute-done | bytes 589856 | tf_op jit(solution)/shard_map/ppermute | solution.py:44
  126.9 5.0 %collective-permute-start.19 = (f32[160,1536]{1,0:T(8,128)S(1)}, f32[160,1536]{1,0:T(8,128)S(1)}, u32[]{:S(2)}, u32[]{:S(2)}) collective-permute-start(f32[160,1536]{1,0:T(8,128)S(1)} %solve.1.refs_1_), channel_id=1, source_target_pairs={{0,96},{1,97},{2,98},{3,99},{4,100},{5,101},{6,102},{7,103},{8,104... | collective-permute-start | bytes 2949128 | tf_op jit(solution)/shard_map/ppermute | solution.py:44
  135.2 3.3 %collective-permute-done.33 = f32[3,96,512]{2,1,0:T(8,128)S(1)} collective-permute-done((f32[3,96,512]{2,1,0:T(8,128)}, f32[3,96,512]{2,1,0:T(8,128)S(1)}, u32[]{:S(2)}, u32[]{:S(2)}) %collective-permute-start.33) | collective-permute-done | bytes 589856 | tf_op jit(solution)/shard_map/ppermute | solution.py:44
  140.3 10.9 %collective-permute-done.19.refs_2_.refs_4_ = f32[160,1536]{1,0:T(8,128)S(1)} collective-permute-done((f32[160,1536]{1,0:T(8,128)S(1)}, f32[160,1536]{1,0:T(8,128)S(1)}, u32[]{:S(2)}, u32[]{:S(2)}) %collective-permute-start.19) | collective-permute-done | bytes 983072 | tf_op jit(solution)/shard_map/ppermute | solution.py:44
  151.3 3.4 %collective-permute-done.18.refs_1_.refs_3_ = f32[160,1536]{1,0:T(8,128)S(1)} collective-permute-done((f32[160,1536]{1,0:T(8,128)S(1)}, f32[160,1536]{1,0:T(8,128)S(1)}, u32[]{:S(2)}, u32[]{:S(2)}) %collective-permute-start.18) | collective-permute-done | bytes 983072 | tf_op jit(solution)/shard_map/ppermute | solution.py:44
  155.0 1.9 collective-permute-start.20
  159.0 3.1 %factor.1 = (bf16[1536,1536]{1,0:T(8,128)(2,1)S(1)}, bf16[1536,1536]{1,0:T(8,128)(2,1)S(1)}) custom-call(s32[6]{0:T(128)S(1)} %stack.93.where_ref.refs_0_, f32[3,3,96,512]{3,2,1,0:T(8,128)S(1)} %pad_maximum_fusion.refs_0_, f32[3,3,96,512]{3,2,1,0:T(8,128)S(1)} %collective-permute-done.27.refs_1_, f32[3,3,96,512]{3,2,1,0:T(8,128)S(1)} %pad_maximum_fusion.1.refs_2_, ...), custom_call_target="tpu_custom_call" | custom-call | flops 9437184 | bytes 18874368 | tf_op jit(solution)/shard_map/factor/pallas_call | solution.py:177
  162.1 2.2 %copy-done.2 = bf16[1536,1536]{1,0:T(8,128)(2,1)} copy-done((bf16[1536,1536]{1,0:T(8,128)(2,1)}, bf16[1536,1536]{1,0:T(8,128)(2,1)S(1)}, u32[]{:S(2)}) %copy-start.2) | copy-done | bytes 4718616
  164.3 9.1 %update.3 = (f32[1536,1280]{1,0:T(8,128)}, f32[192,1280]{1,0:T(8,128)}) custom-call(s32[6]{0:T(128)S(1)} %stack.93.where_ref.refs_0_, f32[160,1536]{1,0:T(8,128)S(1)} %solve.1.refs_1_, f32[160,1536]{1,0:T(8,128)S(1)} %collective-permute-done.17.refs_2_, bf16[1536,1536]{1,0:T(8,128)(2,1)S(1)} %get-tuple-element.10.refs_3_.refs_6_.refs_10_, ...), custom_call_target="tpu_custom_call" | custom-call | flops 3623878656 | bytes 12582912 | tf_op jit(solution)/shard_map/update/pallas_call | solution.py:231
  173.4 2.6 %collective-permute-done.20.refs_3_.refs_5_ = f32[160,1536]{1,0:T(8,128)S(1)} collective-permute-done((f32[160,1536]{1,0:T(8,128)S(1)}, f32[160,1536]{1,0:T(8,128)S(1)}, u32[]{:S(2)}, u32[]{:S(2)}) %collective-permute-start.20) | collective-permute-done | bytes 983072 | tf_op jit(solution)/shard_map/ppermute | solution.py:44
  181.1 13.1 %update.4 = (f32[1536,1280]{1,0:T(8,128)}, f32[192,1280]{1,0:T(8,128)}) custom-call(s32[6]{0:T(128)S(1)} %stack.93.where_ref.refs_0_, f32[160,1536]{1,0:T(8,128)S(1)} %collective-permute-done.18.refs_1_.refs_3_, f32[160,1536]{1,0:T(8,128)S(1)} %collective-permute-done.19.refs_2_.refs_4_, ...), custom_call_target="tpu_custom_call", output_to_operand_aliasing={{0}: (9, {}), {1}: (10, {})} | custom-call | flops 7247757312 | bytes 15728640 | tf_op jit(solution)/shard_map/update/pallas_call | solution.py:231
  194.2 14.2 %update.5 = (f32[1536,1280]{1,0:T(8,128)}, f32[192,1280]{1,0:T(8,128)}) custom-call(s32[6]{0:T(128)S(1)} %stack.93.where_ref.refs_0_, f32[160,1536]{1,0:T(8,128)S(1)} %solve.1.refs_1_, f32[160,1536]{1,0:T(8,128)S(1)} %collective-permute-done.17.refs_2_, ...), custom_call_target="tpu_custom_call", output_to_operand_aliasing={{0}: (13, {}), {1}: (14, {})} | custom-call | flops 7247757312 | bytes 15728640 | tf_op jit(solution)/shard_map/update/pallas_call | solution.py:231
  (77 shorter events, 28.9 us)
Async XLA Ops:
  1.7 17.8 %collective-permute-start.1 = (f32[2,32,512]{2,1,0:T(8,128)S(1)}, f32[2,32,512]{2,1,0:T(8,128)S(1)}, u32[]{:S(2)}, u32[]{:S(2)}) collective-permute-start(f32[2,32,512]{2,1,0:T(8,128)S(1)} %get-tuple-element.24), channel_id=1, source_target_pairs={{16,17},{17,20},{18,23},{19,26},{20,29},{32,33},{33,36},{34,39},{3... | collective-permute-start | bytes 393224 | tf_op jit(solution)/shard_map/ppermute | solution.py:44
  3.5 16.0 %collective-permute-start.2 = (f32[2,32,512]{2,1,0:T(8,128)S(1)}, f32[2,32,512]{2,1,0:T(8,128)S(1)}, u32[]{:S(2)}, u32[]{:S(2)}) collective-permute-start(f32[2,32,512]{2,1,0:T(8,128)S(1)} %get-tuple-element.25), channel_id=1, source_target_pairs={{16,18},{17,21},{18,24},{19,27},{20,30},{32,34},{33,37},{34,40},{3... | collective-permute-start | bytes 393224 | tf_op jit(solution)/shard_map/ppermute | solution.py:44
  9.5 9.9 %collective-permute-start = (f32[2,32,512]{2,1,0:T(8,128)S(1)}, f32[2,32,512]{2,1,0:T(8,128)S(1)}, u32[]{:S(2)}, u32[]{:S(2)}) collective-permute-start(f32[2,32,512]{2,1,0:T(8,128)S(1)} %get-tuple-element.26), channel_id=1, source_target_pairs={{16,16},{17,19},{18,22},{19,25},{20,28},{21,31},{32,32},{33,35},{3... | collective-permute-start | bytes 393224 | tf_op jit(solution)/shard_map/ppermute | solution.py:44
  15.7 87.1 %all-to-all-start = ((f32[8,160,512]{2,1,0:T(8,128)}), f32[8,160,512]{2,1,0:T(8,128)S(1)}, u32[]{:S(2)}, u32[]{:S(2)}) async-start(f32[8,160,512]{2,1,0:T(8,128)} %turn.1), calls=%async_computation | async-start | bytes 5242880 | tf_op jit(solution)/shard_map/all_to_all | solution.py:299
  19.6 31.8 %collective-permute-start.3 = (f32[96,512]{1,0:T(8,128)S(1)}, f32[96,512]{1,0:T(8,128)S(1)}, u32[]{:S(2)}, u32[]{:S(2)}) collective-permute-start(f32[96,512]{1,0:T(8,128)S(1)} %pad_maximum_fusion.9), channel_id=1, source_target_pairs={{16,0},{17,1},{18,2},{19,3},{20,4},{21,5},{22,6},{23,7},{24,8},{25... | collective-permute-start | bytes 589832 | tf_op jit(solution)/shard_map/ppermute | solution.py:44
  51.4 10.6 %collective-permute-start.6 = (f32[96,512]{1,0:T(8,128)S(1)}, f32[96,512]{1,0:T(8,128)S(1)}, u32[]{:S(2)}, u32[]{:S(2)}) collective-permute-start(f32[96,512]{1,0:T(8,128)S(1)} %fusion.1), channel_id=1, source_target_pairs={{0,96},{1,97},{2,98},{3,99},{4,100},{5,101},{6,102},{7,103},{8,104... | collective-permute-start | bytes 589832 | tf_op jit(solution)/shard_map/ppermute | solution.py:44
  53.3 8.6 %collective-permute-start.5 = (f32[96,512]{1,0:T(8,128)S(1)}, f32[96,512]{1,0:T(8,128)S(1)}, u32[]{:S(2)}, u32[]{:S(2)}) collective-permute-start(f32[96,512]{1,0:T(8,128)S(1)} %fusion.1), channel_id=1, source_target_pairs={{0,64},{1,65},{2,66},{3,67},{4,68},{5,69},{6,70},{7,71},{8,72},{9,... | collective-permute-start | bytes 589832 | tf_op jit(solution)/shard_map/ppermute | solution.py:44
  54.6 9.8 %collective-permute-start.4 = (f32[96,512]{1,0:T(8,128)S(1)}, f32[96,512]{1,0:T(8,128)S(1)}, u32[]{:S(2)}, u32[]{:S(2)}) collective-permute-start(f32[96,512]{1,0:T(8,128)S(1)} %fusion.1), channel_id=1, source_target_pairs={{0,32},{1,33},{2,34},{3,35},{4,36},{5,37},{6,38},{7,39},{8,40},{9,... | collective-permute-start | bytes 589832 | tf_op jit(solution)/shard_map/ppermute | solution.py:44
  66.5 8.5 %collective-permute-start.8 = (f32[96,512]{1,0:T(8,128)S(1)}, f32[96,512]{1,0:T(8,128)S(1)}, u32[]{:S(2)}, u32[]{:S(2)}) collective-permute-start(f32[96,512]{1,0:T(8,128)S(1)} %add_add_fusion), channel_id=1, source_target_pairs={{0,12},{1,13},{2,14},{3,15},{4,0},{5,1},{6,2},{7,3},{8,4},{9,5},{1... | collective-permute-start | bytes 589832 | tf_op jit(solution)/shard_map/ppermute | solution.py:44
  66.5 8.6 %collective-permute-start.7 = (f32[96,512]{1,0:T(8,128)S(1)}, f32[96,512]{1,0:T(8,128)S(1)}, u32[]{:S(2)}, u32[]{:S(2)}) collective-permute-start(f32[96,512]{1,0:T(8,128)S(1)} %add_add_fusion), channel_id=1, source_target_pairs={{0,4},{1,5},{2,6},{3,7},{4,8},{5,9},{6,10},{7,11},{8,12},{9,13},{1... | collective-permute-start | bytes 589832 | tf_op jit(solution)/shard_map/ppermute | solution.py:44
  68.5 29.3 %collective-permute-start.28 = (f32[3,96,512]{2,1,0:T(8,128)}, f32[3,96,512]{2,1,0:T(8,128)}, u32[]{:S(2)}, u32[]{:S(2)}) collective-permute-start(f32[3,96,512]{2,1,0:T(8,128)} %param.4), channel_id=1, source_target_pairs={{0,2},{1,3},{2,0},{3,1},{4,6},{5,7},{6,4},{7,5},{8,10},{9,11},{10,... | collective-permute-start | bytes 1769480 | tf_op jit(solution)/shard_map/ppermute | solution.py:44
  73.0 9.0 %collective-permute-start.11 = (f32[96,512]{1,0:T(8,128)S(1)}, f32[96,512]{1,0:T(8,128)S(1)}, u32[]{:S(2)}, u32[]{:S(2)}) collective-permute-start(f32[96,512]{1,0:T(8,128)S(1)} %collective-permute-done.10), channel_id=1, source_target_pairs={{0,4},{1,5},{2,6},{3,7},{4,8},{5,9},{6,10},{7,11},{8,12},{9,13},{1... | collective-permute-start | bytes 589832 | tf_op jit(solution)/shard_map/ppermute | solution.py:44
  75.0 22.8 %collective-permute-start.25 = (f32[3,96,512]{2,1,0:T(8,128)}, f32[3,96,512]{2,1,0:T(8,128)}, u32[]{:S(2)}, u32[]{:S(2)}) collective-permute-start(f32[3,96,512]{2,1,0:T(8,128)} %param.4), channel_id=1, source_target_pairs={{0,4},{1,5},{2,6},{3,7},{4,8},{5,9},{6,10},{7,11},{8,12},{9,13},{1... | collective-permute-start | bytes 1769480 | tf_op jit(solution)/shard_map/ppermute | solution.py:44
  75.0 21.4 %collective-permute-start.14 = (f32[96,512]{1,0:T(8,128)S(1)}, f32[96,512]{1,0:T(8,128)S(1)}, u32[]{:S(2)}, u32[]{:S(2)}) collective-permute-start(f32[96,512]{1,0:T(8,128)S(1)} %collective-permute-done.7), channel_id=1, source_target_pairs={{0,4},{1,5},{2,6},{3,7},{4,8},{5,9},{6,10},{7,11},{8,12},{9,13},{1... | collective-permute-start | bytes 589832 | tf_op jit(solution)/shard_map/ppermute | solution.py:44
  78.6 20.5 %collective-permute-start.9 = (f32[3,96,512]{2,1,0:T(8,128)S(1)}, f32[3,96,512]{2,1,0:T(8,128)S(1)}, u32[]{:S(2)}, u32[]{:S(2)}) collective-permute-start(f32[3,96,512]{2,1,0:T(8,128)S(1)} %pad_maximum_fusion.6.refs_0_), channel_id=1, source_target_pairs={{0,1},{1,0},{2,3},{3,2},{4,5},{5,4},{6,7},{7,6},{8,9},{9,8},{10,11... | collective-permute-start | bytes 1769480 | tf_op jit(solution)/shard_map/ppermute | solution.py:44
  82.0 14.5 %collective-permute-start.15 = (f32[96,512]{1,0:T(8,128)S(1)}, f32[96,512]{1,0:T(8,128)S(1)}, u32[]{:S(2)}, u32[]{:S(2)}) collective-permute-start(f32[96,512]{1,0:T(8,128)S(1)} %collective-permute-done.12), channel_id=1, source_target_pairs={{0,12},{1,13},{2,14},{3,15},{4,0},{5,1},{6,2},{7,3},{8,4},{9,5},{1... | collective-permute-start | bytes 589832 | tf_op jit(solution)/shard_map/ppermute | solution.py:44
  97.8 16.5 %collective-permute-start.30 = (f32[3,96,512]{2,1,0:T(8,128)}, f32[3,96,512]{2,1,0:T(8,128)}, u32[]{:S(2)}, u32[]{:S(2)}) collective-permute-start(f32[3,96,512]{2,1,0:T(8,128)} %collective-permute-done.28), channel_id=1, source_target_pairs={{0,12},{1,13},{2,14},{3,15},{4,0},{5,1},{6,2},{7,3},{8,4},{9,5},{1... | collective-permute-start | bytes 1769480 | tf_op jit(solution)/shard_map/ppermute | solution.py:44
  97.8 29.1 %collective-permute-start.26 = (f32[3,96,512]{2,1,0:T(8,128)}, f32[3,96,512]{2,1,0:T(8,128)}, u32[]{:S(2)}, u32[]{:S(2)}) collective-permute-start(f32[3,96,512]{2,1,0:T(8,128)} %param.4), channel_id=1, source_target_pairs={{0,12},{1,13},{2,14},{3,15},{4,0},{5,1},{6,2},{7,3},{8,4},{9,5},{1... | collective-permute-start | bytes 1769480 | tf_op jit(solution)/shard_map/ppermute | solution.py:44
  100.0 31.9 %collective-permute-start.32 = (f32[3,96,512]{2,1,0:T(8,128)}, f32[3,96,512]{2,1,0:T(8,128)}, u32[]{:S(2)}, u32[]{:S(2)}) collective-permute-start(f32[3,96,512]{2,1,0:T(8,128)} %collective-permute-done.25), channel_id=1, source_target_pairs={{0,4},{1,5},{2,6},{3,7},{4,8},{5,9},{6,10},{7,11},{8,12},{9,13},{1... | collective-permute-start | bytes 1769480 | tf_op jit(solution)/shard_map/ppermute | solution.py:44
  100.8 32.7 %collective-permute-start.29 = (f32[3,96,512]{2,1,0:T(8,128)}, f32[3,96,512]{2,1,0:T(8,128)}, u32[]{:S(2)}, u32[]{:S(2)}) collective-permute-start(f32[3,96,512]{2,1,0:T(8,128)} %collective-permute-done.28), channel_id=1, source_target_pairs={{0,4},{1,5},{2,6},{3,7},{4,8},{5,9},{6,10},{7,11},{8,12},{9,13},{1... | collective-permute-start | bytes 1769480 | tf_op jit(solution)/shard_map/ppermute | solution.py:44
  111.0 28.6 %collective-permute-start.17 = (f32[160,1536]{1,0:T(8,128)S(1)}, f32[160,1536]{1,0:T(8,128)S(1)}, u32[]{:S(2)}, u32[]{:S(2)}) collective-permute-start(f32[160,1536]{1,0:T(8,128)S(1)} %solve.1.refs_1_), channel_id=1, source_target_pairs={{0,16},{1,17},{2,18},{3,19},{4,20},{5,21},{6,22},{7,23},{8,24},{9,... | collective-permute-start | bytes 2949128 | tf_op jit(solution)/shard_map/ppermute | solution.py:44
  114.3 24.2 %collective-permute-start.33 = (f32[3,96,512]{2,1,0:T(8,128)}, f32[3,96,512]{2,1,0:T(8,128)S(1)}, u32[]{:S(2)}, u32[]{:S(2)}) collective-permute-start(f32[3,96,512]{2,1,0:T(8,128)} %collective-permute-done.30), channel_id=1, source_target_pairs={{0,12},{1,13},{2,14},{3,15},{4,0},{5,1},{6,2},{7,3},{8,4},{9,5},{1... | collective-permute-start | bytes 1769480 | tf_op jit(solution)/shard_map/ppermute | solution.py:44
  126.9 24.3 %collective-permute-start.19 = (f32[160,1536]{1,0:T(8,128)S(1)}, f32[160,1536]{1,0:T(8,128)S(1)}, u32[]{:S(2)}, u32[]{:S(2)}) collective-permute-start(f32[160,1536]{1,0:T(8,128)S(1)} %solve.1.refs_1_), channel_id=1, source_target_pairs={{0,96},{1,97},{2,98},{3,99},{4,100},{5,101},{6,102},{7,103},{8,104... | collective-permute-start | bytes 2949128 | tf_op jit(solution)/shard_map/ppermute | solution.py:44
  131.9 22.8 %collective-permute-start.18 = (f32[160,1536]{1,0:T(8,128)S(1)}, f32[160,1536]{1,0:T(8,128)S(1)}, u32[]{:S(2)}, u32[]{:S(2)}) collective-permute-start(f32[160,1536]{1,0:T(8,128)S(1)} %solve.1.refs_1_), channel_id=1, source_target_pairs={{0,32},{1,33},{2,34},{3,35},{4,36},{5,37},{6,38},{7,39},{8,40},{9,... | collective-permute-start | bytes 2949128 | tf_op jit(solution)/shard_map/ppermute | solution.py:44
  133.5 23.8 %collective-permute-start.27 = (f32[3,3,96,512]{3,2,1,0:T(8,128)S(1)}, f32[3,3,96,512]{3,2,1,0:T(8,128)S(1)}, u32[]{:S(2)}, u32[]{:S(2)}) collective-permute-start(f32[3,3,96,512]{3,2,1,0:T(8,128)S(1)} %pad_maximum_fusion.refs_0_), channel_id=1, source_target_pairs={{0,1},{1,0},{2,3},{3,2},{4,5},{5,4},{6,7},{7,6},{8,9},{9,8},{10,11... | collective-permute-start | bytes 5308424 | tf_op jit(solution)/shard_map/ppermute | solution.py:44
  138.5 20.5 %collective-permute-start.31 = (f32[3,3,96,512]{3,2,1,0:T(8,128)S(1)}, f32[3,3,96,512]{3,2,1,0:T(8,128)S(1)}, u32[]{:S(2)}, u32[]{:S(2)}) collective-permute-start(f32[3,3,96,512]{3,2,1,0:T(8,128)S(1)} %pad_maximum_fusion.1.refs_2_), channel_id=1, source_target_pairs={{0,1},{1,0},{2,3},{3,2},{4,5},{5,4},{6,7},{7,6},{8,9},{9,8},{10,11... | collective-permute-start | bytes 5308424 | tf_op jit(solution)/shard_map/ppermute | solution.py:44
  139.7 19.3 %collective-permute-start.34 = (f32[2,3,96,512]{3,2,1,0:T(8,128)S(1)}, f32[2,3,96,512]{3,2,1,0:T(8,128)S(1)}, u32[]{:S(2)}, u32[]{:S(2)}) collective-permute-start(f32[2,3,96,512]{3,2,1,0:T(8,128)S(1)} %pad_maximum_fusion.2.refs_4_), channel_id=1, source_target_pairs={{0,1},{1,0},{2,3},{3,2},{4,5},{5,4},{6,7},{7,6},{8,9},{9,8},{10,11... | collective-permute-start | bytes 3538952 | tf_op jit(solution)/shard_map/ppermute | solution.py:44
  155.0 20.9 %collective-permute-start.20 = (f32[160,1536]{1,0:T(8,128)S(1)}, f32[160,1536]{1,0:T(8,128)S(1)}, u32[]{:S(2)}, u32[]{:S(2)}) collective-permute-start(f32[160,1536]{1,0:T(8,128)S(1)} %get-tuple-element.28), channel_id=1, source_target_pairs={{0,16},{1,17},{2,18},{3,19},{4,20},{5,21},{6,22},{7,23},{8,24},{9,... | collective-permute-start | bytes 2949128 | tf_op jit(solution)/shard_map/ppermute | solution.py:44
  157.0 22.8 %collective-permute-start.22 = (f32[160,1536]{1,0:T(8,128)S(1)}, f32[160,1536]{1,0:T(8,128)S(1)}, u32[]{:S(2)}, u32[]{:S(2)}) collective-permute-start(f32[160,1536]{1,0:T(8,128)S(1)} %get-tuple-element.27), channel_id=1, source_target_pairs={{0,96},{1,97},{2,98},{3,99},{4,100},{5,101},{6,102},{7,103},{8,104... | collective-permute-start | bytes 2949128 | tf_op jit(solution)/shard_map/ppermute | solution.py:44
  157.3 23.8 %collective-permute-start.21 = (f32[160,1536]{1,0:T(8,128)S(1)}, f32[160,1536]{1,0:T(8,128)S(1)}, u32[]{:S(2)}, u32[]{:S(2)}) collective-permute-start(f32[160,1536]{1,0:T(8,128)S(1)} %get-tuple-element.29), channel_id=1, source_target_pairs={{0,32},{1,33},{2,34},{3,35},{4,36},{5,37},{6,38},{7,39},{8,40},{9,... | collective-permute-start | bytes 2949128 | tf_op jit(solution)/shard_map/ppermute | solution.py:44
  176.0 18.2 %collective-permute-start.24 = (f32[80,1536]{1,0:T(8,128)S(1)}, f32[80,1536]{1,0:T(8,128)S(1)}, u32[]{:S(2)}, u32[]{:S(2)}) collective-permute-start(f32[80,1536]{1,0:T(8,128)S(1)} %get-tuple-element.20), channel_id=1, source_target_pairs={{0,96},{1,97},{2,98},{3,99},{4,100},{5,101},{6,102},{7,103},{8,104... | collective-permute-start | bytes 1474568 | tf_op jit(solution)/shard_map/ppermute | solution.py:44
  176.7 17.5 %collective-permute-start.23 = (f32[80,1536]{1,0:T(8,128)S(1)}, f32[80,1536]{1,0:T(8,128)S(1)}, u32[]{:S(2)}, u32[]{:S(2)}) collective-permute-start(f32[80,1536]{1,0:T(8,128)S(1)} %get-tuple-element.21), channel_id=1, source_target_pairs={{0,32},{1,33},{2,34},{3,35},{4,36},{5,37},{6,38},{7,39},{8,40},{9,... | collective-permute-start | bytes 1474568 | tf_op jit(solution)/shard_map/ppermute | solution.py:44
  (10 other events, 50.1 us)

commit v2 on v1

--- a/solution.py
+++ b/solution.py
@@ -103,29 +103,40 @@
             yield ref.at[i], lax.rem(y + step, 4) * 4 + z * 2 + c
 
 
-def turn_kernel(b_ref, o_ref):
-    for d in range(8):
-        o_ref[d, :MAIN] = b_ref[:, MAIN * d : MAIN * d + MAIN].T
-    rest = b_ref[:, 8 * MAIN :].T
-    for d in range(8):
-        o_ref[d, MAIN:] = rest[REST * d : REST * d + REST]
-
-
-def turn(right_side):
+def turn_kernel(where_ref, b_ref, *refs):
+    outs, rest = refs[:-1], refs[-1]
+    rest[...] = b_ref[:, 8 * MAIN :].T
+    for k, out in enumerate(outs):
+        d = lax.rem(where_ref[0] + k, 8)
+        out[:MAIN] = b_ref[:, pl.ds(pl.multiple_of(MAIN * d, MAIN), MAIN)].T
+        out[MAIN:] = rest[pl.ds(pl.multiple_of(REST * d, REST), REST), :]
+
+
+def turn(where, right_side):
+    piece = jax.ShapeDtypeStruct((PIECE, NB), jnp.float32)
     return pl.pallas_call(
         turn_kernel,
         grid=(1,),
-        out_shape=jax.ShapeDtypeStruct((8, PIECE, NB), jnp.float32),
-        in_specs=[pl.BlockSpec((NB, 1280), lambda i: (0, 0))],
-        out_specs=pl.BlockSpec((8, PIECE, NB), lambda i: (0, 0, 0)),
+        out_shape=(piece,) * 8,
+        in_specs=[SMEM, pl.BlockSpec((NB, 1280), lambda i: (0, 0))],
+        out_specs=(pl.BlockSpec((PIECE, NB), lambda i: (0, 0)),) * 8,
+        scratch_shapes=[pltpu.VMEM((8 * REST, NB), jnp.float32)],
         compiler_params=pltpu.CompilerParams(vmem_limit_bytes=20 << 20),
         cost_estimate=pl.CostEstimate(flops=0, bytes_accessed=5 << 20, transcendentals=0),
         name="turn",
-    )(right_side)
-
-
-def solve_kernel(where_ref, pieces_ref, *refs):
-    groups, (inverse_ref, y_ref, wh, wl) = refs[:6], refs[6:]
+    )(where, right_side)
+
+
+def solve_kernel(where_ref, *refs):
+    shifted, groups, (inverse_ref, y_ref, raw, wh, wl) = refs[:8], refs[8:14], refs[14:]
+    for r in range(PANELS):
+        back = lax.rem(where_ref[0] + 8 - r, 8)
+        for k, ref in enumerate(shifted):
+
+            @pl.when(back == k)
+            def _():
+                raw[r] = ref[...]
+
     for ref, s in members(where_ref, groups):
         rows = pl.ds(pl.multiple_of(s * 32, 32), 32)
         for k in range(3):
@@ -133,13 +144,13 @@
             wh[k, rows, :] = hi
             wl[k, rows, :] = lo
     window = lambda k: (wh[k], wl[k])
-    y0 = dot3(split(pieces_ref[0]), split(inverse_ref[0]))
+    y0 = dot3(split(raw[0]), split(inverse_ref[0]))
     y_ref[:, :NB] = y0
     y0 = split(y0)
-    y1 = dot3(split(pieces_ref[1] - dot3(y0, window(0))), split(inverse_ref[1]))
+    y1 = dot3(split(raw[1] - dot3(y0, window(0))), split(inverse_ref[1]))
     y_ref[:, NB : 2 * NB] = y1
     y1 = split(y1)
-    rest = pieces_ref[2] - dot3(y0, window(1)) - dot3(y1, window(2))
+    rest = raw[2] - dot3(y0, window(1)) - dot3(y1, window(2))
     y_ref[:, 2 * NB :] = dot3(split(rest), split(inverse_ref[2]))
 
 
@@ -149,13 +160,13 @@
         solve_kernel,
         grid=(1,),
         out_shape=jax.ShapeDtypeStruct((PIECE, DEPTH), jnp.float32),
-        in_specs=[SMEM, pl.BlockSpec((3, PIECE, NB), lambda i: (0, 0, 0))] + [whole(p) for p in (*groups, inverse_blocks)],
+        in_specs=[SMEM] + [whole(p) for p in (*pieces, *groups, inverse_blocks)],
         out_specs=pl.BlockSpec((PIECE, DEPTH), lambda i: (0, 0)),
-        scratch_shapes=[pltpu.VMEM((3, NB, NB), jnp.bfloat16)] * 2,
-        compiler_params=pltpu.CompilerParams(vmem_limit_bytes=30 << 20),
+        scratch_shapes=[pltpu.VMEM((3, PIECE, NB), jnp.float32)] + [pltpu.VMEM((3, NB, NB), jnp.bfloat16)] * 2,
+        compiler_params=pltpu.CompilerParams(vmem_limit_bytes=34 << 20),
         cost_estimate=pl.CostEstimate(flops=36 * PIECE * NB * NB, bytes_accessed=9 << 20, transcendentals=0),
         name="solve",
-    )(where, pieces, *groups, inverse_blocks)
+    )(where, *pieces, *groups, inverse_blocks)
 
 
 def factor_kernel(where_ref, *refs):
@@ -295,8 +306,9 @@
     window = over_sim(rows)
     factor = prepare_factor(where, over_sim(lower_panels))
 
-    payload = turn(right_side)
-    pieces = lax.all_to_all(payload, "row", 0, 0)
+    turned = turn(where, right_side)
+    shift = lambda k: [(r * 16 + s, (r + k) % 8 * 16 + s) for r in range(PANELS) for s in range(16)]
+    pieces = [turned[0]] + [send(turned[k], shift(k)) for k in range(1, 8)]
     mine = solve(where, pieces, window, inverse_blocks)
 
     left, right, beside = send(mine, X_UP), send(mine, X_DOWN), send(mine, Z_SWAP)

time: 209 us -> 193 us (0.923)
  the two profiles are of different devices: /device:TPU:32 before, /device:TPU:40 now
where the time goes in v2:
time: 193 us
  waiting for transfers between devices  71.8 us (37%)
  starting transfers between devices  66.9 us (35%)
  Pallas kernels  45.3 us (23%)
  local copies, waits for them, and re-layouts  6.76 us (4%)
    ppermute x42, waiting for transfers between devices, send(): return lax.ppermute(array, AXES, pairs)  71.8 us
    ppermute x42, starting transfers between devices, send(): return lax.ppermute(array, AXES, pairs)  66.9 us
    pallas_call x3, Pallas kernels, update(): pl.pallas_call(body, out_shape=(jax.ShapeDtypeStruct((1536, 1280), jnp.fl...  36.3 us
    unnamed x10, local copies, waits for them, and re-layouts  5.41 us
    pallas_call x1, Pallas kernels, solve(): pl.pallas_call(solve_kernel, grid=(1,), out_shape=jax.ShapeDtypeStruct((P...  4.61 us
  transfers between devices with their start and end apart: 42, of which 20 were waited for; matrix products, arithmetic and copies ran while one was open for 1% of the time, Pallas kernels for 16%

profile of v2, /device:TPU:40, one launch (start us, length us, event | category | flops | bytes accessed | tf_op | source)
XLA Modules:
  0.0 192.8 jit_solution(3093847934085818907)
XLA Ops:
  1.7 3.6 %collective-permute-start.8 = (f32[2,32,512]{2,1,0:T(8,128)S(1)}, f32[2,32,512]{2,1,0:T(8,128)S(1)}, u32[]{:S(2)}, u32[]{:S(2)}) collective-permute-start(f32[2,32,512]{2,1,0:T(8,128)S(1)} %get-tuple-element.40), channel_id=1, source_target_pairs={{16,17},{17,20},{18,23},{19,26},{20,29},{32,33},{33,36},{34,39},{3... | collective-permute-start | bytes 393224 | tf_op jit(solution)/shard_map/ppermute | solution.py:44
  5.3 3.6 %collective-permute-start.9 = (f32[2,32,512]{2,1,0:T(8,128)S(1)}, f32[2,32,512]{2,1,0:T(8,128)S(1)}, u32[]{:S(2)}, u32[]{:S(2)}) collective-permute-start(f32[2,32,512]{2,1,0:T(8,128)S(1)} %get-tuple-element.41), channel_id=1, source_target_pairs={{16,18},{17,21},{18,24},{19,27},{20,30},{32,34},{33,37},{34,40},{3... | collective-permute-start | bytes 393224 | tf_op jit(solution)/shard_map/ppermute | solution.py:44
  10.3 2.1 %collective-permute-done.9 = f32[2,32,512]{2,1,0:T(8,128)S(1)} collective-permute-done((f32[2,32,512]{2,1,0:T(8,128)S(1)}, f32[2,32,512]{2,1,0:T(8,128)S(1)}, u32[]{:S(2)}, u32[]{:S(2)}) %collective-permute-start.9) | collective-permute-done | bytes 131104 | tf_op jit(solution)/shard_map/ppermute | solution.py:44
  15.3 3.2 %copy-done = f32[1536,1280]{1,0:T(8,128)S(1)} copy-done((f32[1536,1280]{1,0:T(8,128)S(1)}, f32[1536,1280]{1,0:T(8,128)}, u32[]{:S(2)}) %copy-start) | copy-done | bytes 7864344
  19.9 3.8 %collective-permute-start = (f32[160,512]{1,0:T(8,128)S(1)}, f32[160,512]{1,0:T(8,128)S(1)}, u32[]{:S(2)}, u32[]{:S(2)}) collective-permute-start(f32[160,512]{1,0:T(8,128)S(1)} %get-tuple-element.19), channel_id=1, source_target_pairs={{0,16},{1,17},{2,18},{3,19},{4,20},{5,21},{6,22},{7,23},{8,24},{9,... | collective-permute-start | bytes 983048 | tf_op jit(solution)/shard_map/ppermute | solution.py:44
  23.8 1.9 collective-permute-start.13
  27.0 3.9 %collective-permute-start.11 = (f32[96,512]{1,0:T(8,128)S(1)}, f32[96,512]{1,0:T(8,128)S(1)}, u32[]{:S(2)}, u32[]{:S(2)}) collective-permute-start(f32[96,512]{1,0:T(8,128)S(1)} %fusion.1), channel_id=1, source_target_pairs={{0,32},{1,33},{2,34},{3,35},{4,36},{5,37},{6,38},{7,39},{8,40},{9,... | collective-permute-start | bytes 589832 | tf_op jit(solution)/shard_map/ppermute | solution.py:44
  31.0 1.9 %collective-permute-start.1 = (f32[160,512]{1,0:T(8,128)S(1)}, f32[160,512]{1,0:T(8,128)S(1)}, u32[]{:S(2)}, u32[]{:S(2)}) collective-permute-start(f32[160,512]{1,0:T(8,128)S(1)} %get-tuple-element.20), channel_id=1, source_target_pairs={{0,32},{1,33},{2,34},{3,35},{4,36},{5,37},{6,38},{7,39},{8,40},{9,... | collective-permute-start | bytes 983048 | tf_op jit(solution)/shard_map/ppermute | solution.py:44
  36.0 3.4 %collective-permute-start.4 = (f32[160,512]{1,0:T(8,128)S(1)}, f32[160,512]{1,0:T(8,128)S(1)}, u32[]{:S(2)}, u32[]{:S(2)}) collective-permute-start(f32[160,512]{1,0:T(8,128)S(1)} %get-tuple-element.23), channel_id=1, source_target_pairs={{0,80},{1,81},{2,82},{3,83},{4,84},{5,85},{6,86},{7,87},{8,88},{9,... | collective-permute-start | bytes 983048 | tf_op jit(solution)/shard_map/ppermute | solution.py:44
  41.6 5.6 %collective-permute-done.1.refs_2_ = f32[160,512]{1,0:T(8,128)S(1)} collective-permute-done((f32[160,512]{1,0:T(8,128)S(1)}, f32[160,512]{1,0:T(8,128)S(1)}, u32[]{:S(2)}, u32[]{:S(2)}) %collective-permute-start.1) | collective-permute-done | bytes 327712 | tf_op jit(solution)/shard_map/ppermute | solution.py:44
  47.3 2.7 %collective-permute-start.17 = (f32[96,512]{1,0:T(8,128)S(1)}, f32[96,512]{1,0:T(8,128)S(1)}, u32[]{:S(2)}, u32[]{:S(2)}) collective-permute-start(f32[96,512]{1,0:T(8,128)S(1)} %add_add_fusion), channel_id=1, source_target_pairs={{0,2},{1,3},{2,0},{3,1},{4,6},{5,7},{6,4},{7,5},{8,10},{9,11},{10,... | collective-permute-start | bytes 589832 | tf_op jit(solution)/shard_map/ppermute | solution.py:44
  50.0 4.3 %collective-permute-done.2.refs_3_ = f32[160,512]{1,0:T(8,128)S(1)} collective-permute-done((f32[160,512]{1,0:T(8,128)S(1)}, f32[160,512]{1,0:T(8,128)S(1)}, u32[]{:S(2)}, u32[]{:S(2)}) %collective-permute-start.2) | collective-permute-done | bytes 327712 | tf_op jit(solution)/shard_map/ppermute | solution.py:44
  54.3 4.3 %collective-permute-done.3.refs_4_ = f32[160,512]{1,0:T(8,128)S(1)} collective-permute-done((f32[160,512]{1,0:T(8,128)S(1)}, f32[160,512]{1,0:T(8,128)S(1)}, u32[]{:S(2)}, u32[]{:S(2)}) %collective-permute-start.3) | collective-permute-done | bytes 327712 | tf_op jit(solution)/shard_map/ppermute | solution.py:44
  59.5 6.6 %collective-permute-start.35 = (f32[3,96,512]{2,1,0:T(8,128)S(1)}, f32[3,96,512]{2,1,0:T(8,128)S(1)}, u32[]{:S(2)}, u32[]{:S(2)}) collective-permute-start(f32[3,96,512]{2,1,0:T(8,128)S(1)} %copy-done.4), channel_id=1, source_target_pairs={{0,2},{1,3},{2,0},{3,1},{4,6},{5,7},{6,4},{7,5},{8,10},{9,11},{10,... | collective-permute-start | bytes 1769480 | tf_op jit(solution)/shard_map/ppermute | solution.py:44
  66.3 5.8 %collective-permute-start.6 = (f32[160,512]{1,0:T(8,128)S(1)}, f32[160,512]{1,0:T(8,128)S(1)}, u32[]{:S(2)}, u32[]{:S(2)}) collective-permute-start(f32[160,512]{1,0:T(8,128)S(1)} %get-tuple-element.25), channel_id=1, source_target_pairs={{0,112},{1,113},{2,114},{3,115},{4,116},{5,117},{6,118},{7,119},{8... | collective-permute-start | bytes 983048 | tf_op jit(solution)/shard_map/ppermute | solution.py:44
  75.7 2.1 %collective-permute-done.22 = f32[96,512]{1,0:T(8,128)S(1)} collective-permute-done((f32[96,512]{1,0:T(8,128)S(1)}, f32[96,512]{1,0:T(8,128)S(1)}, u32[]{:S(2)}, u32[]{:S(2)}) %collective-permute-start.22) | collective-permute-done | bytes 196640 | tf_op jit(solution)/shard_map/ppermute | solution.py:44
  77.8 6.2 %collective-permute-done.6.refs_7_ = f32[160,512]{1,0:T(8,128)S(1)} collective-permute-done((f32[160,512]{1,0:T(8,128)S(1)}, f32[160,512]{1,0:T(8,128)S(1)}, u32[]{:S(2)}, u32[]{:S(2)}) %collective-permute-start.6) | collective-permute-done | bytes 327712 | tf_op jit(solution)/shard_map/ppermute | solution.py:44
  85.0 2.7 %collective-permute-done.32 = f32[3,96,512]{2,1,0:T(8,128)S(1)} collective-permute-done((f32[3,96,512]{2,1,0:T(8,128)S(1)}, f32[3,96,512]{2,1,0:T(8,128)S(1)}, u32[]{:S(2)}, u32[]{:S(2)}) %collective-permute-start.32) | collective-permute-done | bytes 589856 | tf_op jit(solution)/shard_map/ppermute | solution.py:44
  87.7 2.3 %collective-permute-start.33 = (f32[3,96,512]{2,1,0:T(8,128)S(1)}, f32[3,96,512]{2,1,0:T(8,128)S(1)}, u32[]{:S(2)}, u32[]{:S(2)}) collective-permute-start(f32[3,96,512]{2,1,0:T(8,128)S(1)} %copy-done.4), channel_id=1, source_target_pairs={{0,12},{1,13},{2,14},{3,15},{4,0},{5,1},{6,2},{7,3},{8,4},{9,5},{1... | collective-permute-start | bytes 1769480 | tf_op jit(solution)/shard_map/ppermute | solution.py:44
  90.6 4.6 %solve.1.refs_1_ = f32[160,1536]{1,0:T(8,128)S(1)} custom-call(s32[6]{0:T(128)S(1)} %stack.93.where_ref.refs_0_, f32[160,512]{1,0:T(8,128)S(1)} %get-tuple-element.18.refs_0_, f32[160,512]{1,0:T(8,128)S(1)} %collective-permute-done.refs_1_, f32[160,512]{1,0:T(8,128)S(1)} %collective-permute-done.1.refs_2_, f32[160,512]{1,0:T(8,128)S(1)} %collective-permute-done.2.refs_3_, ...), custom_call_target="tpu_custom_call" | custom-call | flops 1509949440 | bytes 9437184 | tf_op jit(solution)/shard_map/solve/pallas_call | solution.py:159
  95.2 3.4 %collective-permute-start.24 = (f32[160,1536]{1,0:T(8,128)S(1)}, f32[160,1536]{1,0:T(8,128)S(1)}, u32[]{:S(2)}, u32[]{:S(2)}) collective-permute-start(f32[160,1536]{1,0:T(8,128)S(1)} %solve.1.refs_1_), channel_id=1, source_target_pairs={{0,16},{1,17},{2,18},{3,19},{4,20},{5,21},{6,22},{7,23},{8,24},{9,... | collective-permute-start | bytes 2949128 | tf_op jit(solution)/shard_map/ppermute | solution.py:44
  101.2 11.7 %collective-permute-done.33 = f32[3,96,512]{2,1,0:T(8,128)S(1)} collective-permute-done((f32[3,96,512]{2,1,0:T(8,128)S(1)}, f32[3,96,512]{2,1,0:T(8,128)S(1)}, u32[]{:S(2)}, u32[]{:S(2)}) %collective-permute-start.33) | collective-permute-done | bytes 589856 | tf_op jit(solution)/shard_map/ppermute | solution.py:44
  112.9 2.0 %collective-permute-start.25 = (f32[160,1536]{1,0:T(8,128)S(1)}, f32[160,1536]{1,0:T(8,128)S(1)}, u32[]{:S(2)}, u32[]{:S(2)}) collective-permute-start(f32[160,1536]{1,0:T(8,128)S(1)} %solve.1.refs_1_), channel_id=1, source_target_pairs={{0,32},{1,33},{2,34},{3,35},{4,36},{5,37},{6,38},{7,39},{8,40},{9,... | collective-permute-start | bytes 2949128 | tf_op jit(solution)/shard_map/ppermute | solution.py:44
  115.3 9.8 %collective-permute-done.40 = f32[3,96,512]{2,1,0:T(8,128)S(1)} collective-permute-done((f32[3,96,512]{2,1,0:T(8,128)S(1)}, f32[3,96,512]{2,1,0:T(8,128)S(1)}, u32[]{:S(2)}, u32[]{:S(2)}) %collective-permute-start.40) | collective-permute-done | bytes 589856 | tf_op jit(solution)/shard_map/ppermute | solution.py:44
  125.9 9.9 %collective-permute-done.26.refs_2_.refs_4_ = f32[160,1536]{1,0:T(8,128)S(1)} collective-permute-done((f32[160,1536]{1,0:T(8,128)S(1)}, f32[160,1536]{1,0:T(8,128)S(1)}, u32[]{:S(2)}, u32[]{:S(2)}) %collective-permute-start.26) | collective-permute-done | bytes 983072 | tf_op jit(solution)/shard_map/ppermute | solution.py:44
  137.4 4.2 %collective-permute-start.27 = (f32[160,1536]{1,0:T(8,128)S(1)}, f32[160,1536]{1,0:T(8,128)S(1)}, u32[]{:S(2)}, u32[]{:S(2)}) collective-permute-start(f32[160,1536]{1,0:T(8,128)S(1)} %get-tuple-element.44), channel_id=1, source_target_pairs={{0,16},{1,17},{2,18},{3,19},{4,20},{5,21},{6,22},{7,23},{8,24},{9,... | collective-permute-start | bytes 2949128 | tf_op jit(solution)/shard_map/ppermute | solution.py:44
  143.6 3.1 %factor.1 = (bf16[1536,1536]{1,0:T(8,128)(2,1)S(1)}, bf16[1536,1536]{1,0:T(8,128)(2,1)S(1)}) custom-call(s32[6]{0:T(128)S(1)} %stack.93.where_ref.refs_0_, f32[3,3,96,512]{3,2,1,0:T(8,128)S(1)} %pad_maximum_fusion.refs_0_, f32[3,3,96,512]{3,2,1,0:T(8,128)S(1)} %collective-permute-done.34.refs_1_, f32[3,3,96,512]{3,2,1,0:T(8,128)S(1)} %pad_maximum_fusion.1.refs_2_, ...), custom_call_target="tpu_custom_call" | custom-call | flops 9437184 | bytes 18874368 | tf_op jit(solution)/shard_map/factor/pallas_call | solution.py:188
  146.7 2.2 %copy-done.2 = bf16[1536,1536]{1,0:T(8,128)(2,1)} copy-done((bf16[1536,1536]{1,0:T(8,128)(2,1)}, bf16[1536,1536]{1,0:T(8,128)(2,1)S(1)}, u32[]{:S(2)}) %copy-start.2) | copy-done | bytes 4718616
  148.9 9.1 %update.3 = (f32[1536,1280]{1,0:T(8,128)}, f32[192,1280]{1,0:T(8,128)}) custom-call(s32[6]{0:T(128)S(1)} %stack.93.where_ref.refs_0_, f32[160,1536]{1,0:T(8,128)S(1)} %solve.1.refs_1_, f32[160,1536]{1,0:T(8,128)S(1)} %collective-permute-done.24.refs_2_, bf16[1536,1536]{1,0:T(8,128)(2,1)S(1)} %get-tuple-element.26.refs_3_.refs_6_.refs_10_, ...), custom_call_target="tpu_custom_call" | custom-call | flops 3623878656 | bytes 12582912 | tf_op jit(solution)/shard_map/update/pallas_call | solution.py:242
  158.0 3.7 %collective-permute-done.27.refs_3_.refs_5_ = f32[160,1536]{1,0:T(8,128)S(1)} collective-permute-done((f32[160,1536]{1,0:T(8,128)S(1)}, f32[160,1536]{1,0:T(8,128)S(1)}, u32[]{:S(2)}, u32[]{:S(2)}) %collective-permute-start.27) | collective-permute-done | bytes 983072 | tf_op jit(solution)/shard_map/ppermute | solution.py:44
  165.5 13.1 %update.4 = (f32[1536,1280]{1,0:T(8,128)}, f32[192,1280]{1,0:T(8,128)}) custom-call(s32[6]{0:T(128)S(1)} %stack.93.where_ref.refs_0_, f32[160,1536]{1,0:T(8,128)S(1)} %collective-permute-done.25.refs_1_.refs_3_, f32[160,1536]{1,0:T(8,128)S(1)} %collective-permute-done.26.refs_2_.refs_4_, ...), custom_call_target="tpu_custom_call", output_to_operand_aliasing={{0}: (9, {}), {1}: (10, {})} | custom-call | flops 7247757312 | bytes 15728640 | tf_op jit(solution)/shard_map/update/pallas_call | solution.py:242
  178.6 14.2 %update.5 = (f32[1536,1280]{1,0:T(8,128)}, f32[192,1280]{1,0:T(8,128)}) custom-call(s32[6]{0:T(128)S(1)} %stack.93.where_ref.refs_0_, f32[160,1536]{1,0:T(8,128)S(1)} %solve.1.refs_1_, f32[160,1536]{1,0:T(8,128)S(1)} %collective-permute-done.24.refs_2_, ...), custom_call_target="tpu_custom_call", output_to_operand_aliasing={{0}: (13, {}), {1}: (14, {})} | custom-call | flops 7247757312 | bytes 15728640 | tf_op jit(solution)/shard_map/update/pallas_call | solution.py:242
  (87 shorter events, 30.6 us)
Async XLA Ops:
  19.9 13.0 %collective-permute-start = (f32[160,512]{1,0:T(8,128)S(1)}, f32[160,512]{1,0:T(8,128)S(1)}, u32[]{:S(2)}, u32[]{:S(2)}) collective-permute-start(f32[160,512]{1,0:T(8,128)S(1)} %get-tuple-element.19), channel_id=1, source_target_pairs={{0,16},{1,17},{2,18},{3,19},{4,20},{5,21},{6,22},{7,23},{8,24},{9,... | collective-permute-start | bytes 983048 | tf_op jit(solution)/shard_map/ppermute | solution.py:44
  23.8 10.5 %collective-permute-start.13 = (f32[96,512]{1,0:T(8,128)S(1)}, f32[96,512]{1,0:T(8,128)S(1)}, u32[]{:S(2)}, u32[]{:S(2)}) collective-permute-start(f32[96,512]{1,0:T(8,128)S(1)} %fusion.1), channel_id=1, source_target_pairs={{0,96},{1,97},{2,98},{3,99},{4,100},{5,101},{6,102},{7,103},{8,104... | collective-permute-start | bytes 589832 | tf_op jit(solution)/shard_map/ppermute | solution.py:44
  27.0 13.2 %collective-permute-start.11 = (f32[96,512]{1,0:T(8,128)S(1)}, f32[96,512]{1,0:T(8,128)S(1)}, u32[]{:S(2)}, u32[]{:S(2)}) collective-permute-start(f32[96,512]{1,0:T(8,128)S(1)} %fusion.1), channel_id=1, source_target_pairs={{0,32},{1,33},{2,34},{3,35},{4,36},{5,37},{6,38},{7,39},{8,40},{9,... | collective-permute-start | bytes 589832 | tf_op jit(solution)/shard_map/ppermute | solution.py:44
  31.0 16.3 %collective-permute-start.1 = (f32[160,512]{1,0:T(8,128)S(1)}, f32[160,512]{1,0:T(8,128)S(1)}, u32[]{:S(2)}, u32[]{:S(2)}) collective-permute-start(f32[160,512]{1,0:T(8,128)S(1)} %get-tuple-element.20), channel_id=1, source_target_pairs={{0,32},{1,33},{2,34},{3,35},{4,36},{5,37},{6,38},{7,39},{8,40},{9,... | collective-permute-start | bytes 983048 | tf_op jit(solution)/shard_map/ppermute | solution.py:44
  32.9 21.4 %collective-permute-start.2 = (f32[160,512]{1,0:T(8,128)S(1)}, f32[160,512]{1,0:T(8,128)S(1)}, u32[]{:S(2)}, u32[]{:S(2)}) collective-permute-start(f32[160,512]{1,0:T(8,128)S(1)} %get-tuple-element.21), channel_id=1, source_target_pairs={{0,48},{1,49},{2,50},{3,51},{4,52},{5,53},{6,54},{7,55},{8,56},{9,... | collective-permute-start | bytes 983048 | tf_op jit(solution)/shard_map/ppermute | solution.py:44
  34.2 24.4 %collective-permute-start.3 = (f32[160,512]{1,0:T(8,128)S(1)}, f32[160,512]{1,0:T(8,128)S(1)}, u32[]{:S(2)}, u32[]{:S(2)}) collective-permute-start(f32[160,512]{1,0:T(8,128)S(1)} %get-tuple-element.22), channel_id=1, source_target_pairs={{0,64},{1,65},{2,66},{3,67},{4,68},{5,69},{6,70},{7,71},{8,72},{9,... | collective-permute-start | bytes 983048 | tf_op jit(solution)/shard_map/ppermute | solution.py:44
  36.0 23.5 %collective-permute-start.4 = (f32[160,512]{1,0:T(8,128)S(1)}, f32[160,512]{1,0:T(8,128)S(1)}, u32[]{:S(2)}, u32[]{:S(2)}) collective-permute-start(f32[160,512]{1,0:T(8,128)S(1)} %get-tuple-element.23), channel_id=1, source_target_pairs={{0,80},{1,81},{2,82},{3,83},{4,84},{5,85},{6,86},{7,87},{8,88},{9,... | collective-permute-start | bytes 983048 | tf_op jit(solution)/shard_map/ppermute | solution.py:44
  40.2 25.9 %collective-permute-start.5 = (f32[160,512]{1,0:T(8,128)S(1)}, f32[160,512]{1,0:T(8,128)S(1)}, u32[]{:S(2)}, u32[]{:S(2)}) collective-permute-start(f32[160,512]{1,0:T(8,128)S(1)} %get-tuple-element.24), channel_id=1, source_target_pairs={{0,96},{1,97},{2,98},{3,99},{4,100},{5,101},{6,102},{7,103},{8,104... | collective-permute-start | bytes 983048 | tf_op jit(solution)/shard_map/ppermute | solution.py:44
  47.3 11.3 %collective-permute-start.17 = (f32[96,512]{1,0:T(8,128)S(1)}, f32[96,512]{1,0:T(8,128)S(1)}, u32[]{:S(2)}, u32[]{:S(2)}) collective-permute-start(f32[96,512]{1,0:T(8,128)S(1)} %add_add_fusion), channel_id=1, source_target_pairs={{0,2},{1,3},{2,0},{3,1},{4,6},{5,7},{6,4},{7,5},{8,10},{9,11},{10,... | collective-permute-start | bytes 589832 | tf_op jit(solution)/shard_map/ppermute | solution.py:44
  54.3 11.9 %collective-permute-start.14 = (f32[96,512]{1,0:T(8,128)S(1)}, f32[96,512]{1,0:T(8,128)S(1)}, u32[]{:S(2)}, u32[]{:S(2)}) collective-permute-start(f32[96,512]{1,0:T(8,128)S(1)} %add_add_fusion), channel_id=1, source_target_pairs={{0,4},{1,5},{2,6},{3,7},{4,8},{5,9},{6,10},{7,11},{8,12},{9,13},{1... | collective-permute-start | bytes 589832 | tf_op jit(solution)/shard_map/ppermute | solution.py:44
  58.6 13.5 %collective-permute-start.19 = (f32[96,512]{1,0:T(8,128)S(1)}, f32[96,512]{1,0:T(8,128)S(1)}, u32[]{:S(2)}, u32[]{:S(2)}) collective-permute-start(f32[96,512]{1,0:T(8,128)S(1)} %collective-permute-done.17), channel_id=1, source_target_pairs={{0,12},{1,13},{2,14},{3,15},{4,0},{5,1},{6,2},{7,3},{8,4},{9,5},{1... | collective-permute-start | bytes 589832 | tf_op jit(solution)/shard_map/ppermute | solution.py:44
  59.5 24.5 %collective-permute-start.35 = (f32[3,96,512]{2,1,0:T(8,128)S(1)}, f32[3,96,512]{2,1,0:T(8,128)S(1)}, u32[]{:S(2)}, u32[]{:S(2)}) collective-permute-start(f32[3,96,512]{2,1,0:T(8,128)S(1)} %copy-done.4), channel_id=1, source_target_pairs={{0,2},{1,3},{2,0},{3,1},{4,6},{5,7},{6,4},{7,5},{8,10},{9,11},{10,... | collective-permute-start | bytes 1769480 | tf_op jit(solution)/shard_map/ppermute | solution.py:44
  66.3 17.8 %collective-permute-start.6 = (f32[160,512]{1,0:T(8,128)S(1)}, f32[160,512]{1,0:T(8,128)S(1)}, u32[]{:S(2)}, u32[]{:S(2)}) collective-permute-start(f32[160,512]{1,0:T(8,128)S(1)} %get-tuple-element.25), channel_id=1, source_target_pairs={{0,112},{1,113},{2,114},{3,115},{4,116},{5,117},{6,118},{7,119},{8... | collective-permute-start | bytes 983048 | tf_op jit(solution)/shard_map/ppermute | solution.py:44
  72.9 14.7 %collective-permute-start.32 = (f32[3,96,512]{2,1,0:T(8,128)S(1)}, f32[3,96,512]{2,1,0:T(8,128)S(1)}, u32[]{:S(2)}, u32[]{:S(2)}) collective-permute-start(f32[3,96,512]{2,1,0:T(8,128)S(1)} %copy-done.4), channel_id=1, source_target_pairs={{0,4},{1,5},{2,6},{3,7},{4,8},{5,9},{6,10},{7,11},{8,12},{9,13},{1... | collective-permute-start | bytes 1769480 | tf_op jit(solution)/shard_map/ppermute | solution.py:44
  75.7 14.3 %collective-permute-start.16 = (f32[3,96,512]{2,1,0:T(8,128)S(1)}, f32[3,96,512]{2,1,0:T(8,128)S(1)}, u32[]{:S(2)}, u32[]{:S(2)}) collective-permute-start(f32[3,96,512]{2,1,0:T(8,128)S(1)} %pad_maximum_fusion.6.refs_8_), channel_id=1, source_target_pairs={{0,1},{1,0},{2,3},{3,2},{4,5},{5,4},{6,7},{7,6},{8,9},{9,8},{10,11... | collective-permute-start | bytes 1769480 | tf_op jit(solution)/shard_map/ppermute | solution.py:44
  77.8 12.8 %collective-permute-start.20 = (f32[3,96,512]{2,1,0:T(8,128)S(1)}, f32[3,96,512]{2,1,0:T(8,128)S(1)}, u32[]{:S(2)}, u32[]{:S(2)}) collective-permute-start(f32[3,96,512]{2,1,0:T(8,128)S(1)} %pad_maximum_fusion.7.refs_10_), channel_id=1, source_target_pairs={{0,1},{1,0},{2,3},{3,2},{4,5},{5,4},{6,7},{7,6},{8,9},{9,8},{10,11... | collective-permute-start | bytes 1769480 | tf_op jit(solution)/shard_map/ppermute | solution.py:44
  84.1 16.2 %collective-permute-start.37 = (f32[3,96,512]{2,1,0:T(8,128)S(1)}, f32[3,96,512]{2,1,0:T(8,128)S(1)}, u32[]{:S(2)}, u32[]{:S(2)}) collective-permute-start(f32[3,96,512]{2,1,0:T(8,128)S(1)} %collective-permute-done.35), channel_id=1, source_target_pairs={{0,12},{1,13},{2,14},{3,15},{4,0},{5,1},{6,2},{7,3},{8,4},{9,5},{1... | collective-permute-start | bytes 1769480 | tf_op jit(solution)/shard_map/ppermute | solution.py:44
  87.7 25.2 %collective-permute-start.33 = (f32[3,96,512]{2,1,0:T(8,128)S(1)}, f32[3,96,512]{2,1,0:T(8,128)S(1)}, u32[]{:S(2)}, u32[]{:S(2)}) collective-permute-start(f32[3,96,512]{2,1,0:T(8,128)S(1)} %copy-done.4), channel_id=1, source_target_pairs={{0,12},{1,13},{2,14},{3,15},{4,0},{5,1},{6,2},{7,3},{8,4},{9,5},{1... | collective-permute-start | bytes 1769480 | tf_op jit(solution)/shard_map/ppermute | solution.py:44
  90.0 22.9 %collective-permute-start.39 = (f32[3,96,512]{2,1,0:T(8,128)S(1)}, f32[3,96,512]{2,1,0:T(8,128)S(1)}, u32[]{:S(2)}, u32[]{:S(2)}) collective-permute-start(f32[3,96,512]{2,1,0:T(8,128)S(1)} %collective-permute-done.32), channel_id=1, source_target_pairs={{0,4},{1,5},{2,6},{3,7},{4,8},{5,9},{6,10},{7,11},{8,12},{9,13},{1... | collective-permute-start | bytes 1769480 | tf_op jit(solution)/shard_map/ppermute | solution.py:44
  90.0 25.1 %collective-permute-start.36 = (f32[3,96,512]{2,1,0:T(8,128)S(1)}, f32[3,96,512]{2,1,0:T(8,128)S(1)}, u32[]{:S(2)}, u32[]{:S(2)}) collective-permute-start(f32[3,96,512]{2,1,0:T(8,128)S(1)} %collective-permute-done.35), channel_id=1, source_target_pairs={{0,4},{1,5},{2,6},{3,7},{4,8},{5,9},{6,10},{7,11},{8,12},{9,13},{1... | collective-permute-start | bytes 1769480 | tf_op jit(solution)/shard_map/ppermute | solution.py:44
  95.2 30.0 %collective-permute-start.24 = (f32[160,1536]{1,0:T(8,128)S(1)}, f32[160,1536]{1,0:T(8,128)S(1)}, u32[]{:S(2)}, u32[]{:S(2)}) collective-permute-start(f32[160,1536]{1,0:T(8,128)S(1)} %solve.1.refs_1_), channel_id=1, source_target_pairs={{0,16},{1,17},{2,18},{3,19},{4,20},{5,21},{6,22},{7,23},{8,24},{9,... | collective-permute-start | bytes 2949128 | tf_op jit(solution)/shard_map/ppermute | solution.py:44
  100.3 24.8 %collective-permute-start.40 = (f32[3,96,512]{2,1,0:T(8,128)S(1)}, f32[3,96,512]{2,1,0:T(8,128)S(1)}, u32[]{:S(2)}, u32[]{:S(2)}) collective-permute-start(f32[3,96,512]{2,1,0:T(8,128)S(1)} %collective-permute-done.37), channel_id=1, source_target_pairs={{0,12},{1,13},{2,14},{3,15},{4,0},{5,1},{6,2},{7,3},{8,4},{9,5},{1... | collective-permute-start | bytes 1769480 | tf_op jit(solution)/shard_map/ppermute | solution.py:44
  112.9 22.8 %collective-permute-start.26 = (f32[160,1536]{1,0:T(8,128)S(1)}, f32[160,1536]{1,0:T(8,128)S(1)}, u32[]{:S(2)}, u32[]{:S(2)}) collective-permute-start(f32[160,1536]{1,0:T(8,128)S(1)} %solve.1.refs_1_), channel_id=1, source_target_pairs={{0,96},{1,97},{2,98},{3,99},{4,100},{5,101},{6,102},{7,103},{8,104... | collective-permute-start | bytes 2949128 | tf_op jit(solution)/shard_map/ppermute | solution.py:44
  112.9 24.1 %collective-permute-start.25 = (f32[160,1536]{1,0:T(8,128)S(1)}, f32[160,1536]{1,0:T(8,128)S(1)}, u32[]{:S(2)}, u32[]{:S(2)}) collective-permute-start(f32[160,1536]{1,0:T(8,128)S(1)} %solve.1.refs_1_), channel_id=1, source_target_pairs={{0,32},{1,33},{2,34},{3,35},{4,36},{5,37},{6,38},{7,39},{8,40},{9,... | collective-permute-start | bytes 2949128 | tf_op jit(solution)/shard_map/ppermute | solution.py:44
  115.1 26.8 %collective-permute-start.34 = (f32[3,3,96,512]{3,2,1,0:T(8,128)S(1)}, f32[3,3,96,512]{3,2,1,0:T(8,128)S(1)}, u32[]{:S(2)}, u32[]{:S(2)}) collective-permute-start(f32[3,3,96,512]{3,2,1,0:T(8,128)S(1)} %pad_maximum_fusion.refs_0_), channel_id=1, source_target_pairs={{0,1},{1,0},{2,3},{3,2},{4,5},{5,4},{6,7},{7,6},{8,9},{9,8},{10,11... | collective-permute-start | bytes 5308424 | tf_op jit(solution)/shard_map/ppermute | solution.py:44
  125.1 18.5 %collective-permute-start.38 = (f32[3,3,96,512]{3,2,1,0:T(8,128)S(1)}, f32[3,3,96,512]{3,2,1,0:T(8,128)S(1)}, u32[]{:S(2)}, u32[]{:S(2)}) collective-permute-start(f32[3,3,96,512]{3,2,1,0:T(8,128)S(1)} %pad_maximum_fusion.1.refs_2_), channel_id=1, source_target_pairs={{0,1},{1,0},{2,3},{3,2},{4,5},{5,4},{6,7},{7,6},{8,9},{9,8},{10,11... | collective-permute-start | bytes 5308424 | tf_op jit(solution)/shard_map/ppermute | solution.py:44
  125.2 18.4 %collective-permute-start.41 = (f32[2,3,96,512]{3,2,1,0:T(8,128)S(1)}, f32[2,3,96,512]{3,2,1,0:T(8,128)S(1)}, u32[]{:S(2)}, u32[]{:S(2)}) collective-permute-start(f32[2,3,96,512]{3,2,1,0:T(8,128)S(1)} %pad_maximum_fusion.2.refs_4_), channel_id=1, source_target_pairs={{0,1},{1,0},{2,3},{3,2},{4,5},{5,4},{6,7},{7,6},{8,9},{9,8},{10,11... | collective-permute-start | bytes 3538952 | tf_op jit(solution)/shard_map/ppermute | solution.py:44
  137.4 24.2 %collective-permute-start.27 = (f32[160,1536]{1,0:T(8,128)S(1)}, f32[160,1536]{1,0:T(8,128)S(1)}, u32[]{:S(2)}, u32[]{:S(2)}) collective-permute-start(f32[160,1536]{1,0:T(8,128)S(1)} %get-tuple-element.44), channel_id=1, source_target_pairs={{0,16},{1,17},{2,18},{3,19},{4,20},{5,21},{6,22},{7,23},{8,24},{9,... | collective-permute-start | bytes 2949128 | tf_op jit(solution)/shard_map/ppermute | solution.py:44
  141.6 22.7 %collective-permute-start.29 = (f32[160,1536]{1,0:T(8,128)S(1)}, f32[160,1536]{1,0:T(8,128)S(1)}, u32[]{:S(2)}, u32[]{:S(2)}) collective-permute-start(f32[160,1536]{1,0:T(8,128)S(1)} %get-tuple-element.43), channel_id=1, source_target_pairs={{0,96},{1,97},{2,98},{3,99},{4,100},{5,101},{6,102},{7,103},{8,104... | collective-permute-start | bytes 2949128 | tf_op jit(solution)/shard_map/ppermute | solution.py:44
  141.9 23.6 %collective-permute-start.28 = (f32[160,1536]{1,0:T(8,128)S(1)}, f32[160,1536]{1,0:T(8,128)S(1)}, u32[]{:S(2)}, u32[]{:S(2)}) collective-permute-start(f32[160,1536]{1,0:T(8,128)S(1)} %get-tuple-element.45), channel_id=1, source_target_pairs={{0,32},{1,33},{2,34},{3,35},{4,36},{5,37},{6,38},{7,39},{8,40},{9,... | collective-permute-start | bytes 2949128 | tf_op jit(solution)/shard_map/ppermute | solution.py:44
  161.7 16.9 %collective-permute-start.31 = (f32[80,1536]{1,0:T(8,128)S(1)}, f32[80,1536]{1,0:T(8,128)S(1)}, u32[]{:S(2)}, u32[]{:S(2)}) collective-permute-start(f32[80,1536]{1,0:T(8,128)S(1)} %get-tuple-element.36), channel_id=1, source_target_pairs={{0,96},{1,97},{2,98},{3,99},{4,100},{5,101},{6,102},{7,103},{8,104... | collective-permute-start | bytes 1474568 | tf_op jit(solution)/shard_map/ppermute | solution.py:44
  162.4 16.2 %collective-permute-start.30 = (f32[80,1536]{1,0:T(8,128)S(1)}, f32[80,1536]{1,0:T(8,128)S(1)}, u32[]{:S(2)}, u32[]{:S(2)}) collective-permute-start(f32[80,1536]{1,0:T(8,128)S(1)} %get-tuple-element.37), channel_id=1, source_target_pairs={{0,32},{1,33},{2,34},{3,35},{4,36},{5,37},{6,38},{7,39},{8,40},{9,... | collective-permute-start | bytes 1474568 | tf_op jit(solution)/shard_map/ppermute | solution.py:44
  (15 other events, 188.3 us)

commit v3 on v2

--- a/solution.py
+++ b/solution.py
@@ -196,7 +196,7 @@
     )(where, *groups)
 
 
-TILE = 512
+TILE = 768
 
 
 def put(raw, block, first, ref, rows):
@@ -225,13 +225,13 @@
 
 
 def update(blocks, fill, place, where, pieces, factor, right_side, targets):
-    whole = lambda p: pl.BlockSpec(p.shape, lambda i, j, w: (0,) * len(p.shape), pipeline_mode=pl.Buffered(1))
+    part = lambda n, at: pl.BlockSpec((n, DEPTH), lambda i, j, w: (at, 0), pipeline_mode=pl.Buffered(1))
     column = pl.BlockSpec((TILE, 256), lambda i, j, w: (i, place(j, w)))
     once = pl.BlockSpec((192, 256), lambda i, j, w: (0, place(jnp.where(i == 0, j, blocks - 1), w)))
     tall = pl.BlockSpec((TILE, DEPTH), lambda i, j, w: (i, 0))
     body = lambda *refs: update_kernel(fill, *refs)
-    operands = [where, *pieces, *factor, right_side]
-    specs = [whole(p) for p in pieces] + [tall, tall, column]
+    operands = [where, *(p for p, _, _ in pieces), *factor, right_side]
+    specs = [part(n, at) for _, n, at in pieces] + [tall, tall, column]
     aliases = {}
     if targets is None:
         targets = (jnp.zeros((8, 128), jnp.float32),) * 2
@@ -276,22 +276,22 @@
     put(raw, 1, z * MAIN, right, slice(0, MAIN))
     other = (1 - z) * MAIN
     put(raw, 0, other, crossed, slice(0, HALF))
-    put(raw, 0, other + HALF, up, slice(HALF, MAIN))
-    put(raw, 1, other, down, slice(HALF, PIECE))
+    put(raw, 0, other + HALF, up, slice(0, MAIN - HALF))
+    put(raw, 1, other, down, slice(0, HALF))
     put(raw, 1, other + HALF, crossed, slice(HALF, MAIN))
 
 
 def fill_last(where, pieces, raw):
     x, z = where[5], where[1]
-    mine, beside, left, right, crossed, up, down, far_a, far_b = pieces
+    mine, beside, left, right, up_tail, crossed, up, down, far_a, far_b = pieces
     put(raw, 0, z * MAIN, up, slice(0, HALF))
     put(raw, 0, z * MAIN + HALF, down, slice(0, MAIN - HALF))
     other = (1 - z) * MAIN
     put(raw, 0, other, far_a, slice(0, HALF))
     put(raw, 0, other + HALF, far_b, slice(0, MAIN - HALF))
     tails = (
-        (0, 0, mine, MAIN), (0, 1, beside, MAIN), (3, 0, left, MAIN), (1, 0, right, MAIN),
-        (3, 1, up, MAIN), (1, 1, crossed, MAIN), (2, 0, down, MAIN - HALF), (2, 1, far_b, MAIN - HALF),
+        (0, 0, mine, 0), (0, 1, beside, 0), (3, 0, left, 0), (1, 0, right, 0),
+        (3, 1, up_tail, 0), (1, 1, crossed, 0), (2, 0, down, MAIN - HALF), (2, 1, far_b, MAIN - HALF),
     )
     for dx, dz, ref, first in tails:
         owner = lax.rem(x + dx, 4) * 2 + (z if dz == 0 else 1 - z)
@@ -317,14 +317,16 @@
     down = send(jnp.concatenate([right[B], beside[A]], 0), X_DOWN)
     far_a, far_b = send(crossed[A], X_UP), send(crossed[B], X_DOWN)
 
-    done = update(1, fill_near, lambda j, w: w[5], where, (mine, beside), factor, right_side, None)
+    done = update(1, fill_near, lambda j, w: w[5], where, ((mine, MAIN, 0), (beside, MAIN, 0)), factor, right_side, None)
     done = update(
-        2, fill_sides, lambda j, w: lax.rem(w[5] + 3 + 2 * j, 4), where, (left, right, crossed, up, down),
+        2, fill_sides, lambda j, w: lax.rem(w[5] + 3 + 2 * j, 4), where,
+        ((left, MAIN, 0), (right, MAIN, 0), (crossed, MAIN, 0), (up, HALF, 1), (down, HALF, 1)),
         factor, right_side, done,
     )
     done = update(
         2, fill_last, lambda j, w: jnp.where(j == 0, lax.rem(w[5] + 2, 4), 4), where,
-        (mine, beside, left, right, crossed, up, down, far_a, far_b), factor, right_side, done,
+        tuple((p, REST, 4) for p in (mine, beside, left, right, up, crossed))
+        + tuple((p, HALF, 0) for p in (up, down, far_a, far_b)), factor, right_side, done,
     )
     return done[1], done[0]
 

time: 193 us -> 192 us (level)
  no operation moved by 1% of the time
where the time goes in v3:
time: 192 us
  waiting for transfers between devices  71.8 us (37%)
  starting transfers between devices  66.9 us (35%)
  Pallas kernels  44.5 us (23%)
  local copies, waits for them, and re-layouts  6.76 us (4%)
    ppermute x42, waiting for transfers between devices, send(): return lax.ppermute(array, AXES, pairs)  71.8 us
    ppermute x42, starting transfers between devices, send(): return lax.ppermute(array, AXES, pairs)  66.9 us
    pallas_call x3, Pallas kernels, update(): pl.pallas_call(body, out_shape=(jax.ShapeDtypeStruct((1536, 1280), jnp.fl...  35.5 us
    unnamed x10, local copies, waits for them, and re-layouts  5.41 us
    pallas_call x1, Pallas kernels, solve(): pl.pallas_call(solve_kernel, grid=(1,), out_shape=jax.ShapeDtypeStruct((P...  4.61 us
  transfers between devices with their start and end apart: 42, of which 20 were waited for; matrix products, arithmetic and copies ran while one was open for 1% of the time, Pallas kernels for 16%

profile of v3, /device:TPU:40, one launch (start us, length us, event | category | flops | bytes accessed | tf_op | source)
XLA Modules:
  0.0 192.0 jit_solution(6953812662445622099)
XLA Ops:
  1.7 3.6 %collective-permute-start.8 = (f32[2,32,512]{2,1,0:T(8,128)S(1)}, f32[2,32,512]{2,1,0:T(8,128)S(1)}, u32[]{:S(2)}, u32[]{:S(2)}) collective-permute-start(f32[2,32,512]{2,1,0:T(8,128)S(1)} %get-tuple-element.40), channel_id=1, source_target_pairs={{16,17},{17,20},{18,23},{19,26},{20,29},{32,33},{33,36},{34,39},{3... | collective-permute-start | bytes 393224 | tf_op jit(solution)/shard_map/ppermute | solution.py:44
  5.3 3.6 %collective-permute-start.9 = (f32[2,32,512]{2,1,0:T(8,128)S(1)}, f32[2,32,512]{2,1,0:T(8,128)S(1)}, u32[]{:S(2)}, u32[]{:S(2)}) collective-permute-start(f32[2,32,512]{2,1,0:T(8,128)S(1)} %get-tuple-element.41), channel_id=1, source_target_pairs={{16,18},{17,21},{18,24},{19,27},{20,30},{32,34},{33,37},{34,40},{3... | collective-permute-start | bytes 393224 | tf_op jit(solution)/shard_map/ppermute | solution.py:44
  10.3 2.1 %collective-permute-done.9 = f32[2,32,512]{2,1,0:T(8,128)S(1)} collective-permute-done((f32[2,32,512]{2,1,0:T(8,128)S(1)}, f32[2,32,512]{2,1,0:T(8,128)S(1)}, u32[]{:S(2)}, u32[]{:S(2)}) %collective-permute-start.9) | collective-permute-done | bytes 131104 | tf_op jit(solution)/shard_map/ppermute | solution.py:44
  15.3 3.2 %copy-done = f32[1536,1280]{1,0:T(8,128)S(1)} copy-done((f32[1536,1280]{1,0:T(8,128)S(1)}, f32[1536,1280]{1,0:T(8,128)}, u32[]{:S(2)}) %copy-start) | copy-done | bytes 7864344
  19.9 3.8 %collective-permute-start = (f32[160,512]{1,0:T(8,128)S(1)}, f32[160,512]{1,0:T(8,128)S(1)}, u32[]{:S(2)}, u32[]{:S(2)}) collective-permute-start(f32[160,512]{1,0:T(8,128)S(1)} %get-tuple-element.19), channel_id=1, source_target_pairs={{0,16},{1,17},{2,18},{3,19},{4,20},{5,21},{6,22},{7,23},{8,24},{9,... | collective-permute-start | bytes 983048 | tf_op jit(solution)/shard_map/ppermute | solution.py:44
  23.8 1.9 %collective-permute-start.13 = (f32[96,512]{1,0:T(8,128)S(1)}, f32[96,512]{1,0:T(8,128)S(1)}, u32[]{:S(2)}, u32[]{:S(2)}) collective-permute-start(f32[96,512]{1,0:T(8,128)S(1)} %fusion.1), channel_id=1, source_target_pairs={{0,96},{1,97},{2,98},{3,99},{4,100},{5,101},{6,102},{7,103},{8,104... | collective-permute-start | bytes 589832 | tf_op jit(solution)/shard_map/ppermute | solution.py:44
  27.0 3.9 %collective-permute-start.11 = (f32[96,512]{1,0:T(8,128)S(1)}, f32[96,512]{1,0:T(8,128)S(1)}, u32[]{:S(2)}, u32[]{:S(2)}) collective-permute-start(f32[96,512]{1,0:T(8,128)S(1)} %fusion.1), channel_id=1, source_target_pairs={{0,32},{1,33},{2,34},{3,35},{4,36},{5,37},{6,38},{7,39},{8,40},{9,... | collective-permute-start | bytes 589832 | tf_op jit(solution)/shard_map/ppermute | solution.py:44
  31.0 1.9 %collective-permute-start.1 = (f32[160,512]{1,0:T(8,128)S(1)}, f32[160,512]{1,0:T(8,128)S(1)}, u32[]{:S(2)}, u32[]{:S(2)}) collective-permute-start(f32[160,512]{1,0:T(8,128)S(1)} %get-tuple-element.20), channel_id=1, source_target_pairs={{0,32},{1,33},{2,34},{3,35},{4,36},{5,37},{6,38},{7,39},{8,40},{9,... | collective-permute-start | bytes 983048 | tf_op jit(solution)/shard_map/ppermute | solution.py:44
  36.0 3.4 %collective-permute-start.4 = (f32[160,512]{1,0:T(8,128)S(1)}, f32[160,512]{1,0:T(8,128)S(1)}, u32[]{:S(2)}, u32[]{:S(2)}) collective-permute-start(f32[160,512]{1,0:T(8,128)S(1)} %get-tuple-element.23), channel_id=1, source_target_pairs={{0,80},{1,81},{2,82},{3,83},{4,84},{5,85},{6,86},{7,87},{8,88},{9,... | collective-permute-start | bytes 983048 | tf_op jit(solution)/shard_map/ppermute | solution.py:44
  41.6 5.6 %collective-permute-done.1.refs_2_ = f32[160,512]{1,0:T(8,128)S(1)} collective-permute-done((f32[160,512]{1,0:T(8,128)S(1)}, f32[160,512]{1,0:T(8,128)S(1)}, u32[]{:S(2)}, u32[]{:S(2)}) %collective-permute-start.1) | collective-permute-done | bytes 327712 | tf_op jit(solution)/shard_map/ppermute | solution.py:44
  47.3 2.7 %collective-permute-start.17 = (f32[96,512]{1,0:T(8,128)S(1)}, f32[96,512]{1,0:T(8,128)S(1)}, u32[]{:S(2)}, u32[]{:S(2)}) collective-permute-start(f32[96,512]{1,0:T(8,128)S(1)} %add_add_fusion), channel_id=1, source_target_pairs={{0,2},{1,3},{2,0},{3,1},{4,6},{5,7},{6,4},{7,5},{8,10},{9,11},{10,... | collective-permute-start | bytes 589832 | tf_op jit(solution)/shard_map/ppermute | solution.py:44
  50.0 4.3 %collective-permute-done.2.refs_3_ = f32[160,512]{1,0:T(8,128)S(1)} collective-permute-done((f32[160,512]{1,0:T(8,128)S(1)}, f32[160,512]{1,0:T(8,128)S(1)}, u32[]{:S(2)}, u32[]{:S(2)}) %collective-permute-start.2) | collective-permute-done | bytes 327712 | tf_op jit(solution)/shard_map/ppermute | solution.py:44
  54.3 4.3 %collective-permute-done.3.refs_4_ = f32[160,512]{1,0:T(8,128)S(1)} collective-permute-done((f32[160,512]{1,0:T(8,128)S(1)}, f32[160,512]{1,0:T(8,128)S(1)}, u32[]{:S(2)}, u32[]{:S(2)}) %collective-permute-start.3) | collective-permute-done | bytes 327712 | tf_op jit(solution)/shard_map/ppermute | solution.py:44
  59.5 6.6 %collective-permute-start.35 = (f32[3,96,512]{2,1,0:T(8,128)S(1)}, f32[3,96,512]{2,1,0:T(8,128)S(1)}, u32[]{:S(2)}, u32[]{:S(2)}) collective-permute-start(f32[3,96,512]{2,1,0:T(8,128)S(1)} %copy-done.4), channel_id=1, source_target_pairs={{0,2},{1,3},{2,0},{3,1},{4,6},{5,7},{6,4},{7,5},{8,10},{9,11},{10,... | collective-permute-start | bytes 1769480 | tf_op jit(solution)/shard_map/ppermute | solution.py:44
  66.3 5.8 %collective-permute-start.6 = (f32[160,512]{1,0:T(8,128)S(1)}, f32[160,512]{1,0:T(8,128)S(1)}, u32[]{:S(2)}, u32[]{:S(2)}) collective-permute-start(f32[160,512]{1,0:T(8,128)S(1)} %get-tuple-element.25), channel_id=1, source_target_pairs={{0,112},{1,113},{2,114},{3,115},{4,116},{5,117},{6,118},{7,119},{8... | collective-permute-start | bytes 983048 | tf_op jit(solution)/shard_map/ppermute | solution.py:44
  75.7 2.1 %collective-permute-done.22 = f32[96,512]{1,0:T(8,128)S(1)} collective-permute-done((f32[96,512]{1,0:T(8,128)S(1)}, f32[96,512]{1,0:T(8,128)S(1)}, u32[]{:S(2)}, u32[]{:S(2)}) %collective-permute-start.22) | collective-permute-done | bytes 196640 | tf_op jit(solution)/shard_map/ppermute | solution.py:44
  77.8 6.2 %collective-permute-done.6.refs_7_ = f32[160,512]{1,0:T(8,128)S(1)} collective-permute-done((f32[160,512]{1,0:T(8,128)S(1)}, f32[160,512]{1,0:T(8,128)S(1)}, u32[]{:S(2)}, u32[]{:S(2)}) %collective-permute-start.6) | collective-permute-done | bytes 327712 | tf_op jit(solution)/shard_map/ppermute | solution.py:44
  85.0 2.7 %collective-permute-done.32 = f32[3,96,512]{2,1,0:T(8,128)S(1)} collective-permute-done((f32[3,96,512]{2,1,0:T(8,128)S(1)}, f32[3,96,512]{2,1,0:T(8,128)S(1)}, u32[]{:S(2)}, u32[]{:S(2)}) %collective-permute-start.32) | collective-permute-done | bytes 589856 | tf_op jit(solution)/shard_map/ppermute | solution.py:44
  87.7 2.3 %collective-permute-start.33 = (f32[3,96,512]{2,1,0:T(8,128)S(1)}, f32[3,96,512]{2,1,0:T(8,128)S(1)}, u32[]{:S(2)}, u32[]{:S(2)}) collective-permute-start(f32[3,96,512]{2,1,0:T(8,128)S(1)} %copy-done.4), channel_id=1, source_target_pairs={{0,12},{1,13},{2,14},{3,15},{4,0},{5,1},{6,2},{7,3},{8,4},{9,5},{1... | collective-permute-start | bytes 1769480 | tf_op jit(solution)/shard_map/ppermute | solution.py:44
  90.6 4.6 %solve.1.refs_1_ = f32[160,1536]{1,0:T(8,128)S(1)} custom-call(s32[6]{0:T(128)S(1)} %stack.93.where_ref.refs_0_, f32[160,512]{1,0:T(8,128)S(1)} %get-tuple-element.18.refs_0_, f32[160,512]{1,0:T(8,128)S(1)} %collective-permute-done.refs_1_, f32[160,512]{1,0:T(8,128)S(1)} %collective-permute-done.1.refs_2_, f32[160,512]{1,0:T(8,128)S(1)} %collective-permute-done.2.refs_3_, ...), custom_call_target="tpu_custom_call" | custom-call | flops 1509949440 | bytes 9437184 | tf_op jit(solution)/shard_map/solve/pallas_call | solution.py:159
  95.2 3.4 %collective-permute-start.24 = (f32[160,1536]{1,0:T(8,128)S(1)}, f32[160,1536]{1,0:T(8,128)S(1)}, u32[]{:S(2)}, u32[]{:S(2)}) collective-permute-start(f32[160,1536]{1,0:T(8,128)S(1)} %solve.1.refs_1_), channel_id=1, source_target_pairs={{0,16},{1,17},{2,18},{3,19},{4,20},{5,21},{6,22},{7,23},{8,24},{9,... | collective-permute-start | bytes 2949128 | tf_op jit(solution)/shard_map/ppermute | solution.py:44
  101.2 11.7 %collective-permute-done.33 = f32[3,96,512]{2,1,0:T(8,128)S(1)} collective-permute-done((f32[3,96,512]{2,1,0:T(8,128)S(1)}, f32[3,96,512]{2,1,0:T(8,128)S(1)}, u32[]{:S(2)}, u32[]{:S(2)}) %collective-permute-start.33) | collective-permute-done | bytes 589856 | tf_op jit(solution)/shard_map/ppermute | solution.py:44
  112.9 2.0 %collective-permute-start.25 = (f32[160,1536]{1,0:T(8,128)S(1)}, f32[160,1536]{1,0:T(8,128)S(1)}, u32[]{:S(2)}, u32[]{:S(2)}) collective-permute-start(f32[160,1536]{1,0:T(8,128)S(1)} %solve.1.refs_1_), channel_id=1, source_target_pairs={{0,32},{1,33},{2,34},{3,35},{4,36},{5,37},{6,38},{7,39},{8,40},{9,... | collective-permute-start | bytes 2949128 | tf_op jit(solution)/shard_map/ppermute | solution.py:44
  115.3 9.8 %collective-permute-done.40 = f32[3,96,512]{2,1,0:T(8,128)S(1)} collective-permute-done((f32[3,96,512]{2,1,0:T(8,128)S(1)}, f32[3,96,512]{2,1,0:T(8,128)S(1)}, u32[]{:S(2)}, u32[]{:S(2)}) %collective-permute-start.40) | collective-permute-done | bytes 589856 | tf_op jit(solution)/shard_map/ppermute | solution.py:44
  125.9 9.9 %collective-permute-done.26.refs_2_.refs_4_ = f32[160,1536]{1,0:T(8,128)S(1)} collective-permute-done((f32[160,1536]{1,0:T(8,128)S(1)}, f32[160,1536]{1,0:T(8,128)S(1)}, u32[]{:S(2)}, u32[]{:S(2)}) %collective-permute-start.26) | collective-permute-done | bytes 983072 | tf_op jit(solution)/shard_map/ppermute | solution.py:44
  137.4 4.2 %collective-permute-start.28 = (f32[160,1536]{1,0:T(8,128)S(1)}, f32[160,1536]{1,0:T(8,128)S(1)}, u32[]{:S(2)}, u32[]{:S(2)}) collective-permute-start(f32[160,1536]{1,0:T(8,128)S(1)} %get-tuple-element.44), channel_id=1, source_target_pairs={{0,16},{1,17},{2,18},{3,19},{4,20},{5,21},{6,22},{7,23},{8,24},{9,... | collective-permute-start | bytes 2949128 | tf_op jit(solution)/shard_map/ppermute | solution.py:44
  143.6 3.1 %factor.1 = (bf16[1536,1536]{1,0:T(8,128)(2,1)S(1)}, bf16[1536,1536]{1,0:T(8,128)(2,1)S(1)}) custom-call(s32[6]{0:T(128)S(1)} %stack.93.where_ref.refs_0_, f32[3,3,96,512]{3,2,1,0:T(8,128)S(1)} %pad_maximum_fusion.refs_0_, f32[3,3,96,512]{3,2,1,0:T(8,128)S(1)} %collective-permute-done.34.refs_1_, f32[3,3,96,512]{3,2,1,0:T(8,128)S(1)} %pad_maximum_fusion.1.refs_2_, ...), custom_call_target="tpu_custom_call" | custom-call | flops 9437184 | bytes 18874368 | tf_op jit(solution)/shard_map/factor/pallas_call | solution.py:188
  146.7 2.2 %copy-done.2 = bf16[1536,1536]{1,0:T(8,128)(2,1)} copy-done((bf16[1536,1536]{1,0:T(8,128)(2,1)}, bf16[1536,1536]{1,0:T(8,128)(2,1)S(1)}, u32[]{:S(2)}) %copy-start.2) | copy-done | bytes 4718616
  148.9 9.0 %update.3 = (f32[1536,1280]{1,0:T(8,128)}, f32[192,1280]{1,0:T(8,128)}) custom-call(s32[6]{0:T(128)S(1)} %stack.93.where_ref.refs_0_, f32[160,1536]{1,0:T(8,128)S(1)} %solve.1.refs_1_, f32[160,1536]{1,0:T(8,128)S(1)} %collective-permute-done.24.refs_2_, bf16[1536,1536]{1,0:T(8,128)(2,1)S(1)} %get-tuple-element.26.refs_3_.refs_6_.refs_11_, ...), custom_call_target="tpu_custom_call" | custom-call | flops 3623878656 | bytes 12582912 | tf_op jit(solution)/shard_map/update/pallas_call | solution.py:242
  157.9 3.7 %collective-permute-done.28.refs_3_.refs_6_ = f32[160,1536]{1,0:T(8,128)S(1)} collective-permute-done((f32[160,1536]{1,0:T(8,128)S(1)}, f32[160,1536]{1,0:T(8,128)S(1)}, u32[]{:S(2)}, u32[]{:S(2)}) %collective-permute-start.28) | collective-permute-done | bytes 983072 | tf_op jit(solution)/shard_map/ppermute | solution.py:44
  165.5 12.8 %update.4 = (f32[1536,1280]{1,0:T(8,128)}, f32[192,1280]{1,0:T(8,128)}) custom-call(s32[6]{0:T(128)S(1)} %stack.93.where_ref.refs_0_, f32[160,1536]{1,0:T(8,128)S(1)} %collective-permute-done.25.refs_1_.refs_3_, f32[160,1536]{1,0:T(8,128)S(1)} %collective-permute-done.26.refs_2_.refs_4_, ...), custom_call_target="tpu_custom_call", output_to_operand_aliasing={{0}: (9, {}), {1}: (10, {})} | custom-call | flops 7247757312 | bytes 15728640 | tf_op jit(solution)/shard_map/update/pallas_call | solution.py:242
  178.3 13.7 %update.5 = (f32[1536,1280]{1,0:T(8,128)}, f32[192,1280]{1,0:T(8,128)}) custom-call(s32[6]{0:T(128)S(1)} %stack.93.where_ref.refs_0_, f32[160,1536]{1,0:T(8,128)S(1)} %solve.1.refs_1_, f32[160,1536]{1,0:T(8,128)S(1)} %collective-permute-done.24.refs_2_, ...), custom_call_target="tpu_custom_call", output_to_operand_aliasing={{0}: (14, {}), {1}: (15, {})} | custom-call | flops 7247757312 | bytes 15728640 | tf_op jit(solution)/shard_map/update/pallas_call | solution.py:242
  (87 shorter events, 30.6 us)
Async XLA Ops:
  19.9 13.0 %collective-permute-start = (f32[160,512]{1,0:T(8,128)S(1)}, f32[160,512]{1,0:T(8,128)S(1)}, u32[]{:S(2)}, u32[]{:S(2)}) collective-permute-start(f32[160,512]{1,0:T(8,128)S(1)} %get-tuple-element.19), channel_id=1, source_target_pairs={{0,16},{1,17},{2,18},{3,19},{4,20},{5,21},{6,22},{7,23},{8,24},{9,... | collective-permute-start | bytes 983048 | tf_op jit(solution)/shard_map/ppermute | solution.py:44
  23.8 10.5 %collective-permute-start.13 = (f32[96,512]{1,0:T(8,128)S(1)}, f32[96,512]{1,0:T(8,128)S(1)}, u32[]{:S(2)}, u32[]{:S(2)}) collective-permute-start(f32[96,512]{1,0:T(8,128)S(1)} %fusion.1), channel_id=1, source_target_pairs={{0,96},{1,97},{2,98},{3,99},{4,100},{5,101},{6,102},{7,103},{8,104... | collective-permute-start | bytes 589832 | tf_op jit(solution)/shard_map/ppermute | solution.py:44
  27.0 13.2 %collective-permute-start.11 = (f32[96,512]{1,0:T(8,128)S(1)}, f32[96,512]{1,0:T(8,128)S(1)}, u32[]{:S(2)}, u32[]{:S(2)}) collective-permute-start(f32[96,512]{1,0:T(8,128)S(1)} %fusion.1), channel_id=1, source_target_pairs={{0,32},{1,33},{2,34},{3,35},{4,36},{5,37},{6,38},{7,39},{8,40},{9,... | collective-permute-start | bytes 589832 | tf_op jit(solution)/shard_map/ppermute | solution.py:44
  31.0 16.3 %collective-permute-start.1 = (f32[160,512]{1,0:T(8,128)S(1)}, f32[160,512]{1,0:T(8,128)S(1)}, u32[]{:S(2)}, u32[]{:S(2)}) collective-permute-start(f32[160,512]{1,0:T(8,128)S(1)} %get-tuple-element.20), channel_id=1, source_target_pairs={{0,32},{1,33},{2,34},{3,35},{4,36},{5,37},{6,38},{7,39},{8,40},{9,... | collective-permute-start | bytes 983048 | tf_op jit(solution)/shard_map/ppermute | solution.py:44
  32.9 21.4 %collective-permute-start.2 = (f32[160,512]{1,0:T(8,128)S(1)}, f32[160,512]{1,0:T(8,128)S(1)}, u32[]{:S(2)}, u32[]{:S(2)}) collective-permute-start(f32[160,512]{1,0:T(8,128)S(1)} %get-tuple-element.21), channel_id=1, source_target_pairs={{0,48},{1,49},{2,50},{3,51},{4,52},{5,53},{6,54},{7,55},{8,56},{9,... | collective-permute-start | bytes 983048 | tf_op jit(solution)/shard_map/ppermute | solution.py:44
  34.2 24.4 %collective-permute-start.3 = (f32[160,512]{1,0:T(8,128)S(1)}, f32[160,512]{1,0:T(8,128)S(1)}, u32[]{:S(2)}, u32[]{:S(2)}) collective-permute-start(f32[160,512]{1,0:T(8,128)S(1)} %get-tuple-element.22), channel_id=1, source_target_pairs={{0,64},{1,65},{2,66},{3,67},{4,68},{5,69},{6,70},{7,71},{8,72},{9,... | collective-permute-start | bytes 983048 | tf_op jit(solution)/shard_map/ppermute | solution.py:44
  36.0 23.5 %collective-permute-start.4 = (f32[160,512]{1,0:T(8,128)S(1)}, f32[160,512]{1,0:T(8,128)S(1)}, u32[]{:S(2)}, u32[]{:S(2)}) collective-permute-start(f32[160,512]{1,0:T(8,128)S(1)} %get-tuple-element.23), channel_id=1, source_target_pairs={{0,80},{1,81},{2,82},{3,83},{4,84},{5,85},{6,86},{7,87},{8,88},{9,... | collective-permute-start | bytes 983048 | tf_op jit(solution)/shard_map/ppermute | solution.py:44
  40.2 25.9 %collective-permute-start.5 = (f32[160,512]{1,0:T(8,128)S(1)}, f32[160,512]{1,0:T(8,128)S(1)}, u32[]{:S(2)}, u32[]{:S(2)}) collective-permute-start(f32[160,512]{1,0:T(8,128)S(1)} %get-tuple-element.24), channel_id=1, source_target_pairs={{0,96},{1,97},{2,98},{3,99},{4,100},{5,101},{6,102},{7,103},{8,104... | collective-permute-start | bytes 983048 | tf_op jit(solution)/shard_map/ppermute | solution.py:44
  47.3 11.3 %collective-permute-start.17 = (f32[96,512]{1,0:T(8,128)S(1)}, f32[96,512]{1,0:T(8,128)S(1)}, u32[]{:S(2)}, u32[]{:S(2)}) collective-permute-start(f32[96,512]{1,0:T(8,128)S(1)} %add_add_fusion), channel_id=1, source_target_pairs={{0,2},{1,3},{2,0},{3,1},{4,6},{5,7},{6,4},{7,5},{8,10},{9,11},{10,... | collective-permute-start | bytes 589832 | tf_op jit(solution)/shard_map/ppermute | solution.py:44
  54.3 11.9 %collective-permute-start.14 = (f32[96,512]{1,0:T(8,128)S(1)}, f32[96,512]{1,0:T(8,128)S(1)}, u32[]{:S(2)}, u32[]{:S(2)}) collective-permute-start(f32[96,512]{1,0:T(8,128)S(1)} %add_add_fusion), channel_id=1, source_target_pairs={{0,4},{1,5},{2,6},{3,7},{4,8},{5,9},{6,10},{7,11},{8,12},{9,13},{1... | collective-permute-start | bytes 589832 | tf_op jit(solution)/shard_map/ppermute | solution.py:44
  58.6 13.5 %collective-permute-start.19 = (f32[96,512]{1,0:T(8,128)S(1)}, f32[96,512]{1,0:T(8,128)S(1)}, u32[]{:S(2)}, u32[]{:S(2)}) collective-permute-start(f32[96,512]{1,0:T(8,128)S(1)} %collective-permute-done.17), channel_id=1, source_target_pairs={{0,12},{1,13},{2,14},{3,15},{4,0},{5,1},{6,2},{7,3},{8,4},{9,5},{1... | collective-permute-start | bytes 589832 | tf_op jit(solution)/shard_map/ppermute | solution.py:44
  59.5 24.5 %collective-permute-start.35 = (f32[3,96,512]{2,1,0:T(8,128)S(1)}, f32[3,96,512]{2,1,0:T(8,128)S(1)}, u32[]{:S(2)}, u32[]{:S(2)}) collective-permute-start(f32[3,96,512]{2,1,0:T(8,128)S(1)} %copy-done.4), channel_id=1, source_target_pairs={{0,2},{1,3},{2,0},{3,1},{4,6},{5,7},{6,4},{7,5},{8,10},{9,11},{10,... | collective-permute-start | bytes 1769480 | tf_op jit(solution)/shard_map/ppermute | solution.py:44
  66.3 17.8 %collective-permute-start.6 = (f32[160,512]{1,0:T(8,128)S(1)}, f32[160,512]{1,0:T(8,128)S(1)}, u32[]{:S(2)}, u32[]{:S(2)}) collective-permute-start(f32[160,512]{1,0:T(8,128)S(1)} %get-tuple-element.25), channel_id=1, source_target_pairs={{0,112},{1,113},{2,114},{3,115},{4,116},{5,117},{6,118},{7,119},{8... | collective-permute-start | bytes 983048 | tf_op jit(solution)/shard_map/ppermute | solution.py:44
  72.9 14.7 %collective-permute-start.32 = (f32[3,96,512]{2,1,0:T(8,128)S(1)}, f32[3,96,512]{2,1,0:T(8,128)S(1)}, u32[]{:S(2)}, u32[]{:S(2)}) collective-permute-start(f32[3,96,512]{2,1,0:T(8,128)S(1)} %copy-done.4), channel_id=1, source_target_pairs={{0,4},{1,5},{2,6},{3,7},{4,8},{5,9},{6,10},{7,11},{8,12},{9,13},{1... | collective-permute-start | bytes 1769480 | tf_op jit(solution)/shard_map/ppermute | solution.py:44
  75.7 14.3 %collective-permute-start.16 = (f32[3,96,512]{2,1,0:T(8,128)S(1)}, f32[3,96,512]{2,1,0:T(8,128)S(1)}, u32[]{:S(2)}, u32[]{:S(2)}) collective-permute-start(f32[3,96,512]{2,1,0:T(8,128)S(1)} %pad_maximum_fusion.6.refs_8_), channel_id=1, source_target_pairs={{0,1},{1,0},{2,3},{3,2},{4,5},{5,4},{6,7},{7,6},{8,9},{9,8},{10,11... | collective-permute-start | bytes 1769480 | tf_op jit(solution)/shard_map/ppermute | solution.py:44
  77.8 12.8 %collective-permute-start.20 = (f32[3,96,512]{2,1,0:T(8,128)S(1)}, f32[3,96,512]{2,1,0:T(8,128)S(1)}, u32[]{:S(2)}, u32[]{:S(2)}) collective-permute-start(f32[3,96,512]{2,1,0:T(8,128)S(1)} %pad_maximum_fusion.7.refs_10_), channel_id=1, source_target_pairs={{0,1},{1,0},{2,3},{3,2},{4,5},{5,4},{6,7},{7,6},{8,9},{9,8},{10,11... | collective-permute-start | bytes 1769480 | tf_op jit(solution)/shard_map/ppermute | solution.py:44
  84.1 16.2 %collective-permute-start.37 = (f32[3,96,512]{2,1,0:T(8,128)S(1)}, f32[3,96,512]{2,1,0:T(8,128)S(1)}, u32[]{:S(2)}, u32[]{:S(2)}) collective-permute-start(f32[3,96,512]{2,1,0:T(8,128)S(1)} %collective-permute-done.35), channel_id=1, source_target_pairs={{0,12},{1,13},{2,14},{3,15},{4,0},{5,1},{6,2},{7,3},{8,4},{9,5},{1... | collective-permute-start | bytes 1769480 | tf_op jit(solution)/shard_map/ppermute | solution.py:44
  87.7 25.2 %collective-permute-start.33 = (f32[3,96,512]{2,1,0:T(8,128)S(1)}, f32[3,96,512]{2,1,0:T(8,128)S(1)}, u32[]{:S(2)}, u32[]{:S(2)}) collective-permute-start(f32[3,96,512]{2,1,0:T(8,128)S(1)} %copy-done.4), channel_id=1, source_target_pairs={{0,12},{1,13},{2,14},{3,15},{4,0},{5,1},{6,2},{7,3},{8,4},{9,5},{1... | collective-permute-start | bytes 1769480 | tf_op jit(solution)/shard_map/ppermute | solution.py:44
  90.0 22.9 %collective-permute-start.39 = (f32[3,96,512]{2,1,0:T(8,128)S(1)}, f32[3,96,512]{2,1,0:T(8,128)S(1)}, u32[]{:S(2)}, u32[]{:S(2)}) collective-permute-start(f32[3,96,512]{2,1,0:T(8,128)S(1)} %collective-permute-done.32), channel_id=1, source_target_pairs={{0,4},{1,5},{2,6},{3,7},{4,8},{5,9},{6,10},{7,11},{8,12},{9,13},{1... | collective-permute-start | bytes 1769480 | tf_op jit(solution)/shard_map/ppermute | solution.py:44
  90.0 25.1 %collective-permute-start.36 = (f32[3,96,512]{2,1,0:T(8,128)S(1)}, f32[3,96,512]{2,1,0:T(8,128)S(1)}, u32[]{:S(2)}, u32[]{:S(2)}) collective-permute-start(f32[3,96,512]{2,1,0:T(8,128)S(1)} %collective-permute-done.35), channel_id=1, source_target_pairs={{0,4},{1,5},{2,6},{3,7},{4,8},{5,9},{6,10},{7,11},{8,12},{9,13},{1... | collective-permute-start | bytes 1769480 | tf_op jit(solution)/shard_map/ppermute | solution.py:44
  95.2 30.0 %collective-permute-start.24 = (f32[160,1536]{1,0:T(8,128)S(1)}, f32[160,1536]{1,0:T(8,128)S(1)}, u32[]{:S(2)}, u32[]{:S(2)}) collective-permute-start(f32[160,1536]{1,0:T(8,128)S(1)} %solve.1.refs_1_), channel_id=1, source_target_pairs={{0,16},{1,17},{2,18},{3,19},{4,20},{5,21},{6,22},{7,23},{8,24},{9,... | collective-permute-start | bytes 2949128 | tf_op jit(solution)/shard_map/ppermute | solution.py:44
  100.3 24.8 %collective-permute-start.40 = (f32[3,96,512]{2,1,0:T(8,128)S(1)}, f32[3,96,512]{2,1,0:T(8,128)S(1)}, u32[]{:S(2)}, u32[]{:S(2)}) collective-permute-start(f32[3,96,512]{2,1,0:T(8,128)S(1)} %collective-permute-done.37), channel_id=1, source_target_pairs={{0,12},{1,13},{2,14},{3,15},{4,0},{5,1},{6,2},{7,3},{8,4},{9,5},{1... | collective-permute-start | bytes 1769480 | tf_op jit(solution)/shard_map/ppermute | solution.py:44
  112.9 22.8 %collective-permute-start.26 = (f32[160,1536]{1,0:T(8,128)S(1)}, f32[160,1536]{1,0:T(8,128)S(1)}, u32[]{:S(2)}, u32[]{:S(2)}) collective-permute-start(f32[160,1536]{1,0:T(8,128)S(1)} %solve.1.refs_1_), channel_id=1, source_target_pairs={{0,96},{1,97},{2,98},{3,99},{4,100},{5,101},{6,102},{7,103},{8,104... | collective-permute-start | bytes 2949128 | tf_op jit(solution)/shard_map/ppermute | solution.py:44
  112.9 24.1 %collective-permute-start.25 = (f32[160,1536]{1,0:T(8,128)S(1)}, f32[160,1536]{1,0:T(8,128)S(1)}, u32[]{:S(2)}, u32[]{:S(2)}) collective-permute-start(f32[160,1536]{1,0:T(8,128)S(1)} %solve.1.refs_1_), channel_id=1, source_target_pairs={{0,32},{1,33},{2,34},{3,35},{4,36},{5,37},{6,38},{7,39},{8,40},{9,... | collective-permute-start | bytes 2949128 | tf_op jit(solution)/shard_map/ppermute | solution.py:44
  115.1 26.8 %collective-permute-start.34 = (f32[3,3,96,512]{3,2,1,0:T(8,128)S(1)}, f32[3,3,96,512]{3,2,1,0:T(8,128)S(1)}, u32[]{:S(2)}, u32[]{:S(2)}) collective-permute-start(f32[3,3,96,512]{3,2,1,0:T(8,128)S(1)} %pad_maximum_fusion.refs_0_), channel_id=1, source_target_pairs={{0,1},{1,0},{2,3},{3,2},{4,5},{5,4},{6,7},{7,6},{8,9},{9,8},{10,11... | collective-permute-start | bytes 5308424 | tf_op jit(solution)/shard_map/ppermute | solution.py:44
  125.1 18.5 %collective-permute-start.38 = (f32[3,3,96,512]{3,2,1,0:T(8,128)S(1)}, f32[3,3,96,512]{3,2,1,0:T(8,128)S(1)}, u32[]{:S(2)}, u32[]{:S(2)}) collective-permute-start(f32[3,3,96,512]{3,2,1,0:T(8,128)S(1)} %pad_maximum_fusion.1.refs_2_), channel_id=1, source_target_pairs={{0,1},{1,0},{2,3},{3,2},{4,5},{5,4},{6,7},{7,6},{8,9},{9,8},{10,11... | collective-permute-start | bytes 5308424 | tf_op jit(solution)/shard_map/ppermute | solution.py:44
  125.2 18.4 %collective-permute-start.41 = (f32[2,3,96,512]{3,2,1,0:T(8,128)S(1)}, f32[2,3,96,512]{3,2,1,0:T(8,128)S(1)}, u32[]{:S(2)}, u32[]{:S(2)}) collective-permute-start(f32[2,3,96,512]{3,2,1,0:T(8,128)S(1)} %pad_maximum_fusion.2.refs_4_), channel_id=1, source_target_pairs={{0,1},{1,0},{2,3},{3,2},{4,5},{5,4},{6,7},{7,6},{8,9},{9,8},{10,11... | collective-permute-start | bytes 3538952 | tf_op jit(solution)/shard_map/ppermute | solution.py:44
  137.4 24.2 %collective-permute-start.28 = (f32[160,1536]{1,0:T(8,128)S(1)}, f32[160,1536]{1,0:T(8,128)S(1)}, u32[]{:S(2)}, u32[]{:S(2)}) collective-permute-start(f32[160,1536]{1,0:T(8,128)S(1)} %get-tuple-element.44), channel_id=1, source_target_pairs={{0,16},{1,17},{2,18},{3,19},{4,20},{5,21},{6,22},{7,23},{8,24},{9,... | collective-permute-start | bytes 2949128 | tf_op jit(solution)/shard_map/ppermute | solution.py:44
  141.6 22.7 %collective-permute-start.29 = (f32[160,1536]{1,0:T(8,128)S(1)}, f32[160,1536]{1,0:T(8,128)S(1)}, u32[]{:S(2)}, u32[]{:S(2)}) collective-permute-start(f32[160,1536]{1,0:T(8,128)S(1)} %get-tuple-element.43), channel_id=1, source_target_pairs={{0,96},{1,97},{2,98},{3,99},{4,100},{5,101},{6,102},{7,103},{8,104... | collective-permute-start | bytes 2949128 | tf_op jit(solution)/shard_map/ppermute | solution.py:44
  141.9 23.6 %collective-permute-start.27 = (f32[160,1536]{1,0:T(8,128)S(1)}, f32[160,1536]{1,0:T(8,128)S(1)}, u32[]{:S(2)}, u32[]{:S(2)}) collective-permute-start(f32[160,1536]{1,0:T(8,128)S(1)} %get-tuple-element.45), channel_id=1, source_target_pairs={{0,32},{1,33},{2,34},{3,35},{4,36},{5,37},{6,38},{7,39},{8,40},{9,... | collective-permute-start | bytes 2949128 | tf_op jit(solution)/shard_map/ppermute | solution.py:44
  161.7 16.6 %collective-permute-start.31 = (f32[80,1536]{1,0:T(8,128)S(1)}, f32[80,1536]{1,0:T(8,128)S(1)}, u32[]{:S(2)}, u32[]{:S(2)}) collective-permute-start(f32[80,1536]{1,0:T(8,128)S(1)} %get-tuple-element.36), channel_id=1, source_target_pairs={{0,96},{1,97},{2,98},{3,99},{4,100},{5,101},{6,102},{7,103},{8,104... | collective-permute-start | bytes 1474568 | tf_op jit(solution)/shard_map/ppermute | solution.py:44
  162.4 15.9 %collective-permute-start.30 = (f32[80,1536]{1,0:T(8,128)S(1)}, f32[80,1536]{1,0:T(8,128)S(1)}, u32[]{:S(2)}, u32[]{:S(2)}) collective-permute-start(f32[80,1536]{1,0:T(8,128)S(1)} %get-tuple-element.37), channel_id=1, source_target_pairs={{0,32},{1,33},{2,34},{3,35},{4,36},{5,37},{6,38},{7,39},{8,40},{9,... | collective-permute-start | bytes 1474568 | tf_op jit(solution)/shard_map/ppermute | solution.py:44
  (15 other events, 188.3 us)
